TPU v7x, 32 devices: a whole 2x2x4 slice. The times are simulated.
32 devices in a mesh: sec: 2 (over core), cell: 16 (over z, y, x).
Axes of the slice: x: 2, y: 2, z: 4, core: 2. Of those that a mesh axis runs over, the one named last changes fastest.
Arguments:
- elem_disp: float32 [64, 24], P('cell'), may hold values from -0.9 to 0.9
- plastic_strain: float32 [64, 8, 6, 4096], P('cell', 'sec'), may hold values from -0.06 to 0.06
- hardening_var: float32 [64, 8, 4096], P('cell', 'sec'), may hold values from 0 to 0.1
- shear_mod: float32 [64, 8, 4096], P('cell', 'sec'), may hold values from 0.5 to 4
- bulk_mod: float32 [64, 8, 4096], P('cell', 'sec'), may hold values from 1.5 to 8
- yield_stress: float32 [64, 8, 4096], P('cell', 'sec'), may hold values from 0.1 to 0.4
- sat_stress: float32 [64, 8, 4096], P('cell', 'sec'), may hold values from 0.05 to 0.3
- sat_rate: float32 [64, 8, 4096], P('cell', 'sec'), may hold values from 5 to 50
- fft_iters: int32 [64, 8], P('cell', 'sec'), may hold values from 2 to 8, as said below
- rm_iters: int32 [64, 8], P('cell', 'sec'), may hold values from 1 to 3, as said below
- move_flag: int32 [64, 8], P('cell', 'sec'), may hold values from 0 to 1, as said below
Outputs:
- elem_force: float32 [64, 24], P('cell')
- elem_stiff: float32 [64, 576], P('cell')
- point_stress: float32 [64, 8, 6], P('cell', 'sec')
- new_state: float32 [64, 8, 7, 4096], P('cell', 'sec')
- new_props: float32 [64, 8, 5, 4096], P('cell', 'sec')
Inputs may be any that keep to these rules, and one draw needn't show every extreme that they name: `fft_iters`: some cell has exactly 8 FFT iterations and some exactly 2. `rm_iters`: some cell has exactly 3 Newton steps and some exactly 1. move_flag[e, g] equals move_flag[(e + 32) mod 64, g].
All inputs are finite; a program needn't handle non-finite values.
Results may differ from a plain program's by a relative error of at most 0.0003.
Values sent between devices are 32-bit elements; how exact they have to be, the bound alone decides.
No kernel may reach another device: no remote copies, remote signals or barrier semaphores. Data moves between devices by JAX's collectives and lax.ppermute only.
A program may use at most 64 MiB of HBM per device.

v0:
```python
import functools
import math

import jax
import jax.numpy as jnp
import numpy as np
from jax import lax
from jax.experimental import pallas as pl
from jax.experimental.pallas import tpu as pltpu
from jax.sharding import PartitionSpec as P


GRID = 16
PLANE = GRID * GRID
LANES = 128
BATCH = 8
GAUSS = 8
SLOPE = 0.05
top_precision = lax.Precision.HIGHEST
SUMS = 29
LINES = GRID * PLANE // LANES
P_ROWS = 5 * LINES
S_ROWS = 7 * LINES
ROWS = P_ROWS + S_ROWS
EARLY = 6


def strain_table():
    root = 1.0 / math.sqrt(3.0)
    table = np.zeros((8, 6, 24), np.float32)
    for gauss_pt in range(8):
        point = [((gauss_pt >> axis_bit & 1) * 2 - 1) * root for axis_bit in range(3)]
        for node in range(8):
            signs = [(node >> axis_bit & 1) * 2 - 1 for axis_bit in range(3)]
            grads = []
            for axis_bit in range(3):
                factor = 2.0 * signs[axis_bit] / 8.0
                for other in range(3):
                    if other != axis_bit:
                        factor = factor * (1.0 + signs[other] * point[other])
                grads.append(factor)
            table[gauss_pt, 0, 3 * node + 0] = grads[0]
            table[gauss_pt, 1, 3 * node + 1] = grads[1]
            table[gauss_pt, 2, 3 * node + 2] = grads[2]
            table[gauss_pt, 3, 3 * node + 1] = 0.5 * grads[2]
            table[gauss_pt, 3, 3 * node + 2] = 0.5 * grads[1]
            table[gauss_pt, 4, 3 * node + 0] = 0.5 * grads[2]
            table[gauss_pt, 4, 3 * node + 2] = 0.5 * grads[0]
            table[gauss_pt, 5, 3 * node + 0] = 0.5 * grads[1]
            table[gauss_pt, 5, 3 * node + 1] = 0.5 * grads[0]
    return table


def cas_tables():
    index = np.arange(GRID)
    angle = 2.0 * np.pi * (np.outer(index, index) % GRID) / GRID
    plus = np.cos(angle) + np.sin(angle)
    minus = np.cos(angle) - np.sin(angle)
    full = np.stack(
        [np.kron(plus, plus), -np.kron(minus, minus), -np.kron(plus, minus), -np.kron(minus, plus)]
    ).astype(np.float32)
    high = full.astype(jnp.bfloat16)
    low = (full - high.astype(np.float32)).astype(jnp.bfloat16)
    waves = np.sin(2.0 * np.pi * index / GRID)
    wave_y = np.repeat(waves, GRID)
    wave_z = np.tile(waves, GRID)
    squared = waves[:, None] ** 2 + wave_y[None, :] ** 2 + wave_z[None, :] ** 2
    inv_sq = np.where(squared > 0.01, 1.0 / np.maximum(squared, 0.01), 0.0)
    table = np.concatenate([inv_sq, wave_y[None], wave_z[None], np.zeros((6, PLANE))], axis=0)
    return high, low, table.astype(np.float32), [float(w) for w in waves]


def hartley(values):
    count = len(values)
    if count == 1:
        return list(values)
    half = count // 2
    even = hartley(values[0::2])
    odd = hartley(values[1::2])
    low, high = [], []
    for k in range(half):
        other = odd[(-k) % half]
        if k == 0:
            term = odd[0]
        elif 4 * k == count:
            term = other
        elif 8 * k == count:
            term = (odd[k] + other) * math.sqrt(0.5)
        elif 8 * k == 3 * count:
            term = (other - odd[k]) * math.sqrt(0.5)
        else:
            turn = 2.0 * math.pi * k / count
            term = odd[k] * math.cos(turn) + other * math.sin(turn)
        low.append(even[k] + term)
        high.append(even[k] - term)
    return low + high


def pack_kernel(elems, points, first, flag, *refs):
    *sources, order, head = refs
    total = elems * points

    def place(wanted, start):
        def step(cell, at):
            hit = (flag[cell // points, cell % points] > 0) == wanted

            @pl.when(hit)
            def _():
                order[at] = cell
                order[total + 1 + cell] = at

            return at + hit.astype(jnp.int32)

        return lax.fori_loop(0, total, step, start)

    moving = place(True, jnp.int32(0))
    place(False, moving)
    order[total] = moving

    for slot in range(first):
        cell = order[slot]
        at = (cell // points) * (LINES * points) + cell % points
        for row, source in enumerate(sources):
            for part in range(0, LINES, 8):
                head[slot, row * LINES + part : row * LINES + part + 8, :] = source[
                    pl.ds(at + part * points, 8, stride=points), :
                ]


def solve_kernel(
    elems,
    points,
    begin,
    first,
    waves,
    order,
    fft_iters,
    rm_iters,
    disp,
    bmat,
    plastic,
    hard,
    shear,
    bulk,
    base,
    sat,
    rate,
    high,
    low,
    table,
    other,
    after,
    sums,
    rec,
    field,
    work,
    spec,
    part_hi,
    part_lo,
    acc,
):
    total = elems * points
    block = GRID * BATCH
    row_of = lax.broadcasted_iota(jnp.int32, (BATCH, LANES), 0)

    cells = [order[min(begin + slot, total - 1)] for slot in range(BATCH)]

    section = lax.axis_index("sec")

    def fill(slot, carry):
        cell = order[jnp.minimum(begin + slot, total - 1)]
        e_at, g_at = cell // points, cell % points
        for half in range(2):
            for part in range(2):
                near = (part * 16 + half) * points + g_at
                here = part * 64 + slot
                for comp in range(6):
                    at = (e_at * 6 + comp) * (LINES * points) + near
                    rec[half, pl.ds(comp * block + here, 8, stride=BATCH), :] = plastic[
                        pl.ds(at, 8, stride=2 * points), :
                    ]
                for row, source in enumerate((hard, shear, bulk, base, sat, rate)):
                    at = e_at * (LINES * points) + near
                    rec[half, pl.ds((6 + row) * block + here, 8, stride=BATCH), :] = source[
                        pl.ds(at, 8, stride=2 * points), :
                    ]
        value = jnp.sum(bmat[section * points + g_at] * disp[e_at], axis=1, keepdims=True)
        acc[pl.ds(0, 6), pl.ds(slot, 1), :] = jnp.broadcast_to(value, (6, LANES))[:, None, :]
        return carry

    lax.fori_loop(0, BATCH, fill, 0)

    def per_cell(pick, dtype):
        out = jnp.zeros((BATCH, LANES), dtype)
        for slot in range(BATCH):
            out = jnp.where(row_of == slot, pick(slot), out)
        return out

    fft_count = per_cell(lambda s: fft_iters[cells[s] // points, cells[s] % points], jnp.int32)
    rm_count = per_cell(lambda s: rm_iters[cells[s] // points, cells[s] % points], jnp.int32)
    most = functools.reduce(
        jnp.maximum, [fft_iters[c // points, c % points] for c in cells]
    )

    def extremes(row):
        top = bottom = None
        for half in range(2):
            for x in range(GRID):
                value = rec[half, row * block + x * BATCH : row * block + (x + 1) * BATCH, :]
                top = value if top is None else jnp.maximum(top, value)
                bottom = value if bottom is None else jnp.minimum(bottom, value)
        return 0.5 * (
            jnp.max(top, axis=1, keepdims=True) + jnp.min(bottom, axis=1, keepdims=True)
        )

    mu_ref = extremes(7)
    bulk_ref = extremes(8)
    lame_ref = bulk_ref - 2.0 * mu_ref / 3.0
    coupling = jnp.broadcast_to((lame_ref + mu_ref) / (lame_ref + 2.0 * mu_ref), (BATCH, LANES))
    inv_mu = jnp.broadcast_to(1.0 / (mu_ref * (GRID * PLANE)), (BATCH, LANES))

    for comp in range(6):
        value = jnp.concatenate([acc[comp]] * 2, axis=0)

        def start(pair, carry):
            for half in range(2):
                field[half, pl.ds(comp * block + pair * 16, 16), :] = value
            return carry

        lax.fori_loop(0, GRID // 2, start, 0)

    def prepare(pair, carry):
        for half in range(2):
            load = lambda row: rec[half, pl.ds(row * block + pair * 16, 16), :]
            level, mu, sat, rate = load(6), load(7), load(10), load(11)
            decay = jnp.exp(-rate * level)
            rec[half, pl.ds(12 * block + pair * 16, 16), :] = (
                load(9) + sat * (1.0 - decay) + SLOPE * level
            )
            rest = sat * decay
            rec[half, pl.ds(13 * block + pair * 16, 16), :] = rest
            rec[half, pl.ds(14 * block + pair * 16, 16), :] = 1.0 / (
                3.0 * mu + rest * rate + SLOPE
            )
        return carry

    lax.fori_loop(0, GRID // 2, prepare, 0)

    rm_pair = jnp.concatenate([rm_count] * 2, axis=0)
    second, third = rm_pair > 1, rm_pair > 2

    def newton(over, inc, mu3, rest, rate):
        decay = jnp.exp(-rate * inc)
        num = over - mu3 * inc - rest * (1.0 - decay)
        return inc + num / (mu3 + rest * rate * decay)

    def trial(half, pair):
        load = lambda row: rec[half, pl.ds(row * block + pair * 16, 16), :]
        elastic = [
            field[half, pl.ds(comp * block + pair * 16, 16), :] - load(comp) for comp in range(6)
        ]
        volume = elastic[0] + elastic[1] + elastic[2]
        mu = load(7)
        mu2 = 2.0 * mu
        mean = volume * (1.0 / 3.0)
        dev = [mu2 * (part - mean) for part in elastic[:3]] + [mu2 * part for part in elastic[3:]]
        squared = 1.5 * (dev[0] * dev[0] + dev[1] * dev[1] + dev[2] * dev[2]) + 3.0 * (
            dev[3] * dev[3] + dev[4] * dev[4] + dev[5] * dev[5]
        )
        return load, volume, mu, dev, squared

    def increments(load, mu, over):
        mu3 = 3.0 * mu + SLOPE
        rest, rate = load(13), load(11)
        inc = over * load(14)
        inc = jnp.where(second, newton(over, inc, mu3, rest, rate), inc)
        return jnp.where(third, newton(over, inc, mu3, rest, rate), inc)

    def stress_step(pair, carry):
        for half in range(2):
            load, volume, mu, dev, squared = trial(half, pair)
            base = load(9)
            capped = jnp.maximum(squared, base * base)
            inv_eq = lax.rsqrt(capped)
            over = jnp.maximum(capped * inv_eq - load(12), 0.0)
            inc = increments(load, mu, over)
            shrink = 1.0 - 3.0 * mu * inc * inv_eq
            pressure = load(8) * volume
            for comp in range(6):
                value = shrink * dev[comp]
                if comp < 3:
                    value = value + pressure
                upper = value.astype(jnp.bfloat16)
                at = pl.ds(comp * block + pair * 16, 16)
                lanes = slice(half * LANES, (half + 1) * LANES)
                part_hi[at, lanes] = upper
                part_lo[at, lanes] = (value - upper.astype(jnp.float32)).astype(jnp.bfloat16)
        return carry

    def plane_product(store):
        for which, (from_row, rows) in enumerate(
            ((0, 3 * block), (3 * block, block), (4 * block, block), (5 * block, block))
        ):
            for at in range(from_row, from_row + rows, block):
                left_hi = part_hi[at : at + block, :]
                left_lo = part_lo[at : at + block, :]
                dot = functools.partial(jnp.dot, preferred_element_type=jnp.float32)
                store(
                    at,
                    dot(left_hi, high[which])
                    + (dot(left_lo, high[which]) + dot(left_hi, low[which])),
                )

    def store_spec(at, value):
        for half in range(2):
            work[half, at : at + block, :] = value[:, half * LANES : (half + 1) * LANES]

    def update_field(at, value):
        for half in range(2):
            field[half, at : at + block, :] = (
                field[half, at : at + block, :] - value[:, half * LANES : (half + 1) * LANES]
            )

    def flip(comp, k):
        return (-k) % GRID if comp in (4, 5) else k

    def sweep(index, carry):
        lax.fori_loop(0, GRID // 2, stress_step, 0)
        plane_product(store_spec)
        scale_cell = jnp.where(index < fft_count, inv_mu, 0.0)

        def spectral(half, inner):
            for comp in range(6):
                lines = hartley(
                    [
                        work[half, comp * block + x * BATCH : comp * block + (x + 1) * BATCH, :]
                        for x in range(GRID)
                    ]
                )
                for k in range(GRID):
                    at = comp * block + flip(comp, k) * BATCH
                    spec[half, at : at + BATCH, :] = lines[k]
            wave_y = jnp.broadcast_to(table[half, GRID : GRID + 1, :], (BATCH, LANES))
            wave_z = jnp.broadcast_to(table[half, GRID + 1 : GRID + 2, :], (BATCH, LANES))
            for k in range(GRID):
                wave_x = waves[k]
                inv_sq = jnp.broadcast_to(table[half, k : k + 1, :], (BATCH, LANES))
                s = [
                    spec[half, comp * block + k * BATCH : comp * block + (k + 1) * BATCH, :]
                    for comp in range(6)
                ]
                comp_a = s[0] * wave_x + s[5] * wave_y + s[4] * wave_z
                comp_b = s[5] * wave_x + s[1] * wave_y + s[3] * wave_z
                comp_c = s[4] * wave_x + s[3] * wave_y + s[2] * wave_z
                along = (wave_x * comp_a + wave_y * comp_b + wave_z * comp_c) * (
                    inv_sq * coupling
                )
                scale = inv_sq * scale_cell
                vec_a = (comp_a - along * wave_x) * scale
                vec_b = (comp_b - along * wave_y) * scale
                vec_c = (comp_c - along * wave_z) * scale
                mapped = (
                    wave_x * vec_a,
                    wave_y * vec_b,
                    wave_z * vec_c,
                    0.5 * (wave_y * vec_c + wave_z * vec_b),
                    0.5 * (wave_x * vec_c + wave_z * vec_a),
                    0.5 * (wave_x * vec_b + wave_y * vec_a),
                )
                for comp in range(6):
                    at = comp * block + flip(comp, k) * BATCH
                    work[half, at : at + BATCH, :] = mapped[comp]
            return inner

        for half in range(2):
            spectral(half, 0)
            for comp in range(6):
                lines = hartley(
                    [
                        work[half, comp * block + x * BATCH : comp * block + (x + 1) * BATCH, :]
                        for x in range(GRID)
                    ]
                )
                for pair in range(GRID // 2):
                    value = jnp.concatenate([lines[2 * pair], lines[2 * pair + 1]], axis=0)
                    upper = value.astype(jnp.bfloat16)
                    at = comp * block + pair * 16
                    lanes = slice(half * LANES, (half + 1) * LANES)
                    part_hi[at : at + 16, lanes] = upper
                    part_lo[at : at + 16, lanes] = (value - upper.astype(jnp.float32)).astype(
                        jnp.bfloat16
                    )
        plane_product(update_field)
        return carry

    lax.fori_loop(0, most, sweep, 0)

    acc[...] = jnp.zeros_like(acc)

    def finish(pair, carry):
        for half in range(2):
            load, volume, mu, dev, squared = trial(half, pair)
            base = load(9)
            trial_eq = jnp.sqrt(squared)
            excess = trial_eq - load(12)
            over = jnp.maximum(excess, 0.0)
            inc = increments(load, mu, over)
            inv_eq = 1.0 / jnp.maximum(trial_eq, base)
            lost = 3.0 * mu * inc * inv_eq
            shrink = 1.0 - lost
            pressure = load(8) * volume
            grow = 1.5 * inc * inv_eq
            for comp in range(6):
                work[half, pl.ds(comp * block + pair * 16, 16), :] = load(comp) + grow * dev[comp]
            spec[half, pl.ds(pair * 16, 16), :] = load(6) + inc
            rate = load(11)
            slope = load(13) * rate * jnp.exp(-rate * inc) + SLOPE
            corr = jnp.where(excess > 0.0, 3.0 * mu / (3.0 * mu + slope) - lost, 0.0)
            weight = 3.0 * mu * corr * (inv_eq * inv_eq)
            terms = [shrink * part for part in dev]
            terms = [term + pressure for term in terms[:3]] + terms[3:]
            terms.append(load(8))
            terms.append(2.0 * mu * shrink)
            for c in range(6):
                scaled = weight * dev[c]
                for d in range(c, 6):
                    terms.append(scaled * dev[d])
            for at, term in enumerate(terms):
                acc[at] = acc[at] + (term[:BATCH] + term[BATCH:])
        return carry

    lax.fori_loop(0, GRID // 2, finish, 0)

    lane_of = lax.broadcasted_iota(jnp.int32, (BATCH, LANES), 1)
    out = jnp.zeros((BATCH, LANES), jnp.float32)
    for at in range(SUMS):
        out = jnp.where(lane_of == at, jnp.sum(acc[at], axis=1, keepdims=True), out)
    sums[...] = out * (1.0 / (GRID * PLANE))

    ahead = max(begin - first, 0)
    if begin:
        for at in range(ahead):
            after[at] = other[at]
    for slot in range(min(BATCH, total - begin)):
        alone = begin == 0 and slot < first
        target = other if alone else after
        here = slot if alone else begin + slot - first
        for half in range(2):
            for part in range(2):
                near = part * 16 + half
                for row in range(7):
                    source, from_row = (work, row) if row < 6 else (spec, 0)
                    at = (0 if alone else P_ROWS) + row * LINES + near
                    target[here, pl.ds(at, 8, stride=2), :] = source[
                        half, pl.ds(from_row * block + part * 64 + slot, 8, stride=BATCH), :
                    ]
                if not alone:
                    for row in range(5):
                        target[here, pl.ds(row * LINES + near, 8, stride=2), :] = rec[
                            half, pl.ds((7 + row) * block + part * 64 + slot, 8, stride=BATCH), :
                        ]


def merge_kernel(
    elems,
    points,
    first,
    order,
    s_head,
    rem,
    got_p,
    got_s,
    shear,
    bulk,
    base,
    sat,
    rate,
    new_state,
    new_props,
    cells,
    s_out,
    p_out,
    in_sem,
    own_sem,
    out_sem,
):
    total = elems * points
    moving = order[total]
    rows = LINES * points
    state_part = pl.ds(P_ROWS, S_ROWS)

    def own_props(e_at):
        return [
            pltpu.make_async_copy(
                source.at[pl.ds(pl.multiple_of(e_at * rows, 8), rows), :],
                p_out.at[e_at, pl.ds(row * rows, rows), :],
                own_sem.at[e_at],
            )
            for row, source in enumerate((shear, bulk, base, sat, rate))
        ]

    def arrival(cell, act):
        slot = order[total + 1 + cell]
        late = jnp.maximum(slot - first, 0)
        sem = in_sem.at[cell]
        moved, soon = slot < moving, slot < first

        @pl.when(jnp.logical_not(moved) & soon)
        def _():
            act(
                pltpu.make_async_copy(
                    s_head.at[jnp.minimum(slot, first - 1)], cells.at[cell, state_part, :], sem
                )
            )

        @pl.when(jnp.logical_not(soon))
        def _():
            act(pltpu.make_async_copy(rem.at[late], cells.at[cell], sem))

    def leaving(e_at):
        return (
            pltpu.make_async_copy(s_out.at[e_at], new_state.at[e_at], out_sem.at[e_at, 0]),
            pltpu.make_async_copy(p_out.at[e_at], new_props.at[e_at], out_sem.at[e_at, 1]),
        )

    @pl.loop(0, elems)
    def _(e_at):
        for g_at in range(points):
            arrival(e_at * points + g_at, lambda copy: copy.start())
        for copy in own_props(e_at):
            copy.start()

    @pl.loop(0, elems)
    def _(e_at):
        for copy in own_props(e_at):
            copy.wait()

        @pl.loop(0, points)
        def _(g_at):
            cell = e_at * points + g_at
            slot = order[total + 1 + cell]
            arrival(cell, lambda copy: copy.wait())
            moved, soon = slot < moving, slot < first
            early = jnp.minimum(slot, first - 1)

            def put(target, count, load):
                for row in range(count):
                    for part in range(0, LINES, 8):
                        at = row * rows + part * points + g_at
                        target[e_at, pl.ds(at, 8, stride=points), :] = load(row * LINES + part)

            @pl.when(moved & soon)
            def _():
                put(p_out, 5, lambda at: got_p[early, at : at + 8, :])
                put(s_out, 7, lambda at: got_s[early, at : at + 8, :])

            @pl.when(moved & jnp.logical_not(soon))
            def _():
                put(p_out, 5, lambda at: cells[cell, at : at + 8, :])

            @pl.when(jnp.logical_not(moved & soon))
            def _():
                put(s_out, 7, lambda at: cells[cell, P_ROWS + at : P_ROWS + at + 8, :])

        for copy in leaving(e_at):
            copy.start()

    @pl.loop(0, elems)
    def _(e_at):
        for copy in leaving(e_at):
            copy.wait()


def element_terms(table_part, sums, points):
    elems = sums.shape[0] // points
    weights = np.array([1.0, 1.0, 1.0, 2.0, 2.0, 2.0], np.float32)
    stress = sums[:, 0:6]
    block = np.outer([1.0, 1.0, 1.0, 0.0, 0.0, 0.0], [1.0, 1.0, 1.0, 0.0, 0.0, 0.0])
    spread = np.zeros((23, 36), np.float32)
    spread[0] = block.reshape(36)
    spread[1] = (np.eye(6) - block / 3.0).reshape(36)
    at = 2
    for c in range(6):
        for d in range(c, 6):
            spread[at, 6 * c + d] = -weights[d]
            spread[at, 6 * d + c] = -weights[c]
            at += 1
    tangent = jnp.dot(sums[:, 6:SUMS], spread, precision=top_precision)
    stress_part = stress.reshape(elems, points, 6)
    force = (
        jnp.einsum("egc,gcn->en", stress_part * weights, table_part, precision=top_precision)
        / GAUSS
    )
    scaled = tangent.reshape(elems, points, 6, 6) * weights[None, None, :, None]
    stiff = (
        jnp.einsum(
            "gcn,egcd,gdm->enm", table_part, scaled, table_part, precision=top_precision
        ).reshape(elems, 576)
        / GAUSS
    )
    return stress_part, force, stiff


VMEM = pl.BlockSpec(memory_space=pltpu.VMEM)
SMEM = pl.BlockSpec(memory_space=pltpu.SMEM)
ANY = pl.BlockSpec(memory_space=pl.ANY)
GRANT = 60 * 2**20
MERGE_GRANT = 24 * 2**20


def shape(*dims, dtype=jnp.float32):
    return jax.ShapeDtypeStruct(dims, dtype)


def local(
    elem_disp,
    plastic_strain,
    hardening_var,
    shear_mod,
    bulk_mod,
    yield_stress,
    sat_stress,
    sat_rate,
    fft_iters,
    rm_iters,
    move_flag,
):
    elems, points = plastic_strain.shape[:2]
    voxels = plastic_strain.shape[3]
    total = elems * points
    group = min(BATCH, total)
    first = max(1, total * EARLY // 16)
    devices = lax.axis_size("cell")
    route = [((i - devices // 2) % devices, i) for i in range(devices)]

    params = pltpu.CompilerParams(vmem_limit_bytes=GRANT)
    bmat = jnp.asarray(strain_table())

    def flat(array):
        lead = array.shape[2:-1]
        tiles = array.reshape(elems, points, *lead, LINES, LANES)
        return jnp.moveaxis(tiles, 1, -2).reshape(-1, LANES)

    def whole(lines, lead):
        tiles = lines.reshape(elems, lead, LINES, points, LANES)
        return jnp.moveaxis(tiles, 3, 1).reshape(elems, points, lead, voxels)

    props = [flat(a) for a in (shear_mod, bulk_mod, yield_stress, sat_stress, sat_rate)]
    hard, plastic = flat(hardening_var), flat(plastic_strain)
    order, p_head = pl.pallas_call(
        functools.partial(pack_kernel, elems, points, first),
        out_shape=(shape(2 * total + 1, dtype=jnp.int32), shape(first, P_ROWS, LANES)),
        in_specs=[SMEM] + [VMEM] * 5,
        out_specs=(SMEM, VMEM),
        compiler_params=params,
        name="pack",
    )(move_flag, *props)

    got_p = lax.ppermute(p_head, "cell", route)

    high, low, table, waves = cas_tables()
    table = table.reshape(24, 2, LANES).transpose(1, 0, 2)
    block = GRID * BATCH
    disp = elem_disp.reshape(elems, 1, elem_disp.shape[1])

    def solve(begin, count, other=None):
        late = shape(count, ROWS, LANES)
        alone = () if begin else (shape(first, S_ROWS, LANES),)
        return pl.pallas_call(
            functools.partial(solve_kernel, elems, points, begin, first, waves),
            out_shape=alone + (late, shape(BATCH, LANES)),
            in_specs=[SMEM] * 3 + [VMEM] * (13 if begin else 12),
            out_specs=(VMEM,) * (len(alone) + 2),
            scratch_shapes=[
                pltpu.VMEM((2, 15 * block, LANES), jnp.float32),
                pltpu.VMEM((2, 6 * block, LANES), jnp.float32),
                pltpu.VMEM((2, 6 * block, LANES), jnp.float32),
                pltpu.VMEM((2, 6 * block, LANES), jnp.float32),
                pltpu.VMEM((6 * block, PLANE), jnp.bfloat16),
                pltpu.VMEM((6 * block, PLANE), jnp.bfloat16),
                pltpu.VMEM((SUMS, BATCH, LANES), jnp.float32),
            ],
            compiler_params=params,
            cost_estimate=pl.CostEstimate(
                flops=20 * 10**9, bytes_accessed=8 * 10**6, transcendentals=0
            ),
            name="solve",
        )(
            order,
            fft_iters,
            rm_iters,
            disp,
            bmat,
            plastic,
            hard,
            *props,
            high,
            low,
            table,
            *(() if other is None else (other,)),
        )

    s_head, rem, sums = solve(0, group - first)
    got_s = lax.ppermute(s_head, "cell", route)
    if total > group:
        rem, more = solve(group, total - first, rem)
        sums = jnp.concatenate([sums, more], axis=0)

    slots = order[:total]
    place = (slots[None, :] == jnp.arange(total)[:, None]).astype(jnp.float32)
    sums = jnp.dot(place, sums[:total], precision=top_precision)
    table_part = lax.dynamic_slice_in_dim(bmat, lax.axis_index("sec") * points, points, 0)
    stress, force_part, stiff_part = element_terms(table_part, sums, points)
    sections = lax.axis_size("sec")
    force, stiff = force_part, stiff_part
    for step in range(1, sections):
        ring = [((i - step) % sections, i) for i in range(sections)]
        force = force + lax.ppermute(force_part, "sec", ring)
        stiff = stiff + lax.ppermute(stiff_part, "sec", ring)
    rem, force, stiff, stress = lax.optimization_barrier((rem, force, stiff, stress))

    def branch(count):
        def run(cells):
            if count == 0:
                return cells
            got = lax.ppermute(cells[:count], "cell", route)
            return lax.dynamic_update_slice_in_dim(cells, got, 0, 0)

        return run

    extra = jnp.clip(
        jnp.sum((move_flag > 0).astype(jnp.int32)) - first, 0, total - first
    )
    rem = lax.switch(extra, [branch(c) for c in range(total - first + 1)], rem)

    new_state, new_props = pl.pallas_call(
        functools.partial(merge_kernel, elems, points, first),
        out_shape=(
            shape(elems, 7 * LINES * points, LANES),
            shape(elems, 5 * LINES * points, LANES),
        ),
        in_specs=[SMEM] + [ANY] * 2 + [VMEM] * 2 + [ANY] * 5,
        out_specs=(ANY, ANY),
        scratch_shapes=[
            pltpu.VMEM((total, ROWS, LANES), jnp.float32),
            pltpu.VMEM((elems, 7 * LINES * points, LANES), jnp.float32),
            pltpu.VMEM((elems, 5 * LINES * points, LANES), jnp.float32),
            pltpu.SemaphoreType.DMA((total,)),
            pltpu.SemaphoreType.DMA((elems,)),
            pltpu.SemaphoreType.DMA((elems, 2)),
        ],
        compiler_params=pltpu.CompilerParams(vmem_limit_bytes=MERGE_GRANT),
        name="merge",
    )(order, s_head, rem, got_p, got_s, *props)
    return force, stiff, stress, whole(new_state, 7), whole(new_props, 5)


def solution(mesh):
    in_specs = (
        P("cell", None),
        P("cell", "sec", None, None),
        P("cell", "sec", None),
        P("cell", "sec", None),
        P("cell", "sec", None),
        P("cell", "sec", None),
        P("cell", "sec", None),
        P("cell", "sec", None),
        P("cell", "sec"),
        P("cell", "sec"),
        P("cell", "sec"),
    )
    out_specs = (
        P("cell", None),
        P("cell", None),
        P("cell", "sec", None),
        P("cell", "sec", None, None),
        P("cell", "sec", None, None),
    )

    return jax.shard_map(local, mesh=mesh, in_specs=in_specs, out_specs=out_specs, check_vma=False)
```

profile of v0, /device:TPU:2, one launch (start us, length us, event | category | flops | bytes accessed | tf_op | source)
XLA Modules:
  0.0 132.9 jit_solution(11505309167993738460)
XLA Ops:
  0.6 2.7 %pack.1 = (s32[33]{0:T(128)}, f32[6,160,128]{2,1,0:T(8,128)}) custom-call(s32[4,4]{1,0:T(4,128)} %flag.1, f32[512,128]{1,0:T(8,128)} %bitcast.69, f32[512,128]{1,0:T(8,128)} %bitcast.73, f32[512,128]{1,0:T(8,128)} %bitcast.77, f32[512,128]{1,0:T(8,128)} %bitcast.81, f32[512,128]{1,0:T(8,128)} %bitcast.85), custom_call_target="tpu_custom_call" | custom-call | tf_op jit(solution)/shard_map/pack/pallas_call | solution.py:650
  3.3 22.1 %solve.2 = (f32[6,224,128]{2,1,0:T(8,128)}, f32[2,384,128]{2,1,0:T(8,128)}, f32[8,128]{1,0:T(8,128)}) custom-call(s32[33]{0:T(128)} %get-tuple-element.41.order, s32[4,4]{1,0:T(4,128)} %fft_iters.3, s32[4,4]{1,0:T(4,128)} %rm_iters.3, f32[4,1,24]{2,1,0:T(1,128)} %bitcast.98, f32[8,6,24]{2,1,0:T(8,128)} %constant.55.clone.bmat, f32[3072,128]{1,0:T(8,128)} %bitcast.93, ...), custom_call_target="tpu_custom_call" | custom-call | flops 20000000000 | bytes 8000000 | tf_op jit(solution)/shard_map/solve/pallas_call | solution.py:669
  25.5 0.0 copy-start.6
  25.5 0.0 copy-start.11
  25.5 0.0 copy-start.12
  25.5 0.0 copy-start.8
  25.5 0.0 copy-start.5
  25.5 0.0 copy-start.9
  25.5 0.0 copy-start.10
  25.6 22.9 %solve.3 = (f32[10,384,128]{2,1,0:T(8,128)}, f32[8,128]{1,0:T(8,128)}) custom-call(s32[33]{0:T(128)} %get-tuple-element.41.order, s32[4,4]{1,0:T(4,128)} %fft_iters.3, s32[4,4]{1,0:T(4,128)} %rm_iters.3, f32[4,1,24]{2,1,0:T(1,128)} %bitcast.99, f32[8,6,24]{2,1,0:T(8,128)} %constant.55.clone.bmat, f32[3072,128]{1,0:T(8,128)} %bitcast.94, ...), custom_call_target="tpu_custom_call" | custom-call | flops 20000000000 | bytes 8000000 | tf_op jit(solution)/shard_map/solve/pallas_call | solution.py:669
  48.4 0.0 copy-done.6
  48.4 0.0 copy-done.11
  48.5 0.8 fusion.7
  49.3 0.0 copy-done.12
  49.3 0.0 copy-done.8
  49.3 0.2 fusion.1
  49.5 0.0 collective-permute-start.10
  49.5 2.6 %collective-permute-start.12 = (f32[6,160,128]{2,1,0:T(8,128)}, f32[6,160,128]{2,1,0:T(8,128)S(1)}, u32[]{:S(2)}, u32[]{:S(2)}) collective-permute-start(f32[6,160,128]{2,1,0:T(8,128)} %get-tuple-element.51), channel_id=1, source_target_pairs={{8,0},{9,1},{10,2},{11,3},{12,4},{13,5},{14,6},{15,7},{0,8},{1,9},... | collective-permute-start | bytes 1474568 | tf_op jit(solution)/shard_map/ppermute | solution.py:659
  52.1 0.0 copy-done.5
  52.1 0.3 collective-permute-start.13
  52.5 0.0 copy-done.9
  52.5 0.2 fusion.5
  52.7 0.1 reshape.94
  52.8 0.4 convolution_bitcast_fusion
  53.1 0.3 fusion
  53.4 0.1 div.18
  53.5 0.1 collective-permute-start.11
  53.6 0.0 copy-done.10
  53.6 0.6 convert_reduce_fusion
  54.9 0.0 collective-permute-done.10
  54.9 0.6 add.11
  55.5 0.0 collective-permute-done.11
  55.5 0.6 add.12
  56.1 0.0 copy-start.4
  56.1 0.0 copy-done.7
  56.1 72.2 %conditional.1 = (f32[10,384,128]{2,1,0:T(8,128)}) conditional(s32[]{:T(128)} %clamp.3, f32[10,384,128]{2,1,0:T(8,128)} %get-tuple-element.50, f32[10,384,128]{2,1,0:T(8,128)} %get-tuple-element.50, f32[10,384,128]{2,1,0:T(8,128)} %get-tuple-element.50, f32[10,384,128]{2,1,0:T(8,128)} %get-tuple-element.50, ...), branch_computations={%region_1.2_spmd, %region_2.3_spmd, %region_3.4_spmd, %region_4.5_... | conditional | bytes 14155824 | solution.py:734
  56.2 1.2 slice.26
  57.4 2.7 %collective-permute-start.3 = (f32[3,384,128]{2,1,0:T(8,128)S(1)}, f32[3,384,128]{2,1,0:T(8,128)S(1)}, u32[]{:S(2)}, u32[]{:S(2)}) collective-permute-start(f32[3,384,128]{2,1,0:T(8,128)S(1)} %slice.26), channel_id=1, source_target_pairs={{8,0},{9,1},{10,2},{11,3},{12,4},{13,5},{14,6},{15,7},{0,8},{1,9},... | collective-permute-start | bytes 1769480 | tf_op jit(solution)/shard_map/cond/branch_3_fun/ppermute | solution.py:726
  60.0 67.4 %collective-permute-done.3 = f32[3,384,128]{2,1,0:T(8,128)S(1)} collective-permute-done((f32[3,384,128]{2,1,0:T(8,128)S(1)}, f32[3,384,128]{2,1,0:T(8,128)S(1)}, u32[]{:S(2)}, u32[]{:S(2)}) %collective-permute-start.3) | collective-permute-done | bytes 589856 | tf_op jit(solution)/shard_map/cond/branch_3_fun/ppermute | solution.py:726
  127.5 0.9 constant_dynamic-update-slice_fusion.2
  128.3 0.0 collective-permute-done.12.got_p
  128.3 0.0 collective-permute-done.13.got_s
  128.3 0.0 copy-done
  128.3 0.0 copy-done.1
  128.3 0.0 copy-done.2
  128.4 0.0 copy-done.3
  128.4 0.0 copy-done.4
  128.4 4.5 %merge.1 = (f32[4,896,128]{2,1,0:T(8,128)}, f32[4,640,128]{2,1,0:T(8,128)}) custom-call(s32[33]{0:T(128)S(1)} %copy-done.6, f32[6,224,128]{2,1,0:T(8,128)S(1)} %copy-done.5, f32[10,384,128]{2,1,0:T(8,128)} %get-tuple-element.54.rem, f32[6,160,128]{2,1,0:T(8,128)S(1)} %collective-permute-done.12.got_p, f32[6,224,128]{2,1,0:T(8,128)S(1)} %collective-permute-done.13.got_s, ...), custom_call_target="tpu_custom_call" | custom-call | tf_op jit(solution)/shard_map/merge/pallas_call | solution.py:736
  (6 shorter events, 0.0 us)
Async XLA Ops:
  25.5 23.0 %copy-start.6 = (s32[33]{0:T(128)S(1)}, s32[33]{0:T(128)}, u32[]{:S(2)}) copy-start(s32[33]{0:T(128)} %get-tuple-element.41.order) | copy-start | bytes 400
  25.5 23.0 %copy-start.11 = (f32[8,128]{1,0:T(8,128)S(1)}, f32[8,128]{1,0:T(8,128)}, u32[]{:S(2)}) copy-start(f32[8,128]{1,0:T(8,128)} %get-tuple-element.44) | copy-start | bytes 12292
  25.5 23.8 %copy-start.12 = (f32[6]{0:T(128)S(1)}, f32[6]{0:T(128)}, u32[]{:S(2)}) copy-start(f32[6]{0:T(128)} %constant.60.clone) | copy-start | bytes 76
  25.5 23.8 %copy-start.8 = (f32[8,6,24]{2,1,0:T(8,128)S(1)}, f32[8,6,24]{2,1,0:T(8,128)}, u32[]{:S(2)}) copy-start(f32[8,6,24]{2,1,0:T(8,128)} %constant.55.clone.bmat) | copy-start | bytes 13828
  25.5 26.6 %copy-start.5 = (f32[6,224,128]{2,1,0:T(8,128)S(1)}, f32[6,224,128]{2,1,0:T(8,128)}, u32[]{:S(2)}) copy-start(f32[6,224,128]{2,1,0:T(8,128)} %get-tuple-element.49.s_head) | copy-start | bytes 2064388
  25.5 27.0 %copy-start.9 = (f32[23,36]{1,0:T(8,128)S(1)}, f32[23,36]{1,0:T(8,128)}, u32[]{:S(2)}) copy-start(f32[23,36]{1,0:T(8,128)} %constant.59.clone) | copy-start | bytes 9940
  25.5 28.1 %copy-start.10 = (s32[4,4]{1,0:T(4,128)S(1)}, s32[4,4]{1,0:T(4,128)}, u32[]{:S(2)}) copy-start(s32[4,4]{1,0:T(4,128)} %flag.1) | copy-start | bytes 196
  49.3 6.9 %copy-start.7 = (f32[16,128]{1,0:T(8,128)}, f32[16,128]{1,0:T(8,128)S(1)}, u32[]{:S(2)}) copy-start(f32[16,128]{1,0:T(8,128)S(1)} %fusion.7) | copy-start | bytes 24580
  49.5 5.4 %collective-permute-start.10 = (f32[4,24]{1,0:T(4,128)S(1)}, f32[4,24]{1,0:T(4,128)S(1)}, u32[]{:S(2)}, u32[]{:S(2)}) collective-permute-start(f32[4,24]{1,0:T(4,128)S(1)} %fusion.1), channel_id=1, source_target_pairs={{16,0},{0,16},{17,1},{1,17},{18,2},{2,18},{19,3},{3,19},{20,4},{4,... | collective-permute-start | bytes 1160 | tf_op jit(solution)/shard_map/ppermute | solution.py:718
  49.5 78.8 %collective-permute-start.12 = (f32[6,160,128]{2,1,0:T(8,128)}, f32[6,160,128]{2,1,0:T(8,128)S(1)}, u32[]{:S(2)}, u32[]{:S(2)}) collective-permute-start(f32[6,160,128]{2,1,0:T(8,128)} %get-tuple-element.51), channel_id=1, source_target_pairs={{8,0},{9,1},{10,2},{11,3},{12,4},{13,5},{14,6},{15,7},{0,8},{1,9},... | collective-permute-start | bytes 1474568 | tf_op jit(solution)/shard_map/ppermute | solution.py:659
  52.1 76.2 %collective-permute-start.13 = (f32[6,224,128]{2,1,0:T(8,128)S(1)}, f32[6,224,128]{2,1,0:T(8,128)S(1)}, u32[]{:S(2)}, u32[]{:S(2)}) collective-permute-start(f32[6,224,128]{2,1,0:T(8,128)S(1)} %copy-done.5), channel_id=1, source_target_pairs={{8,0},{9,1},{10,2},{11,3},{12,4},{13,5},{14,6},{15,7},{0,8},{1,9},... | collective-permute-start | bytes 2064392 | tf_op jit(solution)/shard_map/ppermute | solution.py:704
  53.5 2.0 %collective-permute-start.11 = (f32[4,576]{1,0:T(4,128)S(1)}, f32[4,576]{1,0:T(4,128)S(1)}, u32[]{:S(2)}, u32[]{:S(2)}) collective-permute-start(f32[4,576]{1,0:T(4,128)S(1)} %div.18), channel_id=1, source_target_pairs={{16,0},{0,16},{17,1},{1,17},{18,2},{2,18},{19,3},{3,19},{20,4},{4,... | collective-permute-start | bytes 27656 | tf_op jit(solution)/shard_map/ppermute | solution.py:719
  56.1 72.2 %copy-start = (f32[4,4,4096]{2,1,0:T(4,128)S(1)}, f32[4,4,4096]{2,1,0:T(4,128)}, u32[]{:S(2)}) copy-start(f32[4,4,4096]{2,1,0:T(4,128)} %param.32) | copy-start | bytes 786436
  56.1 72.3 %copy-start.1 = (f32[4,4,4096]{2,1,0:T(4,128)S(1)}, f32[4,4,4096]{2,1,0:T(4,128)}, u32[]{:S(2)}) copy-start(f32[4,4,4096]{2,1,0:T(4,128)} %param.33) | copy-start | bytes 786436
  56.1 72.3 %copy-start.2 = (f32[4,4,4096]{2,1,0:T(4,128)S(1)}, f32[4,4,4096]{2,1,0:T(4,128)}, u32[]{:S(2)}) copy-start(f32[4,4,4096]{2,1,0:T(4,128)} %param.34) | copy-start | bytes 786436
  56.1 72.3 %copy-start.3 = (f32[4,4,4096]{2,1,0:T(4,128)S(1)}, f32[4,4,4096]{2,1,0:T(4,128)}, u32[]{:S(2)}) copy-start(f32[4,4,4096]{2,1,0:T(4,128)} %param.35) | copy-start | bytes 786436
  56.1 72.3 %copy-start.4 = (f32[4,4,4096]{2,1,0:T(4,128)S(1)}, f32[4,4,4096]{2,1,0:T(4,128)}, u32[]{:S(2)}) copy-start(f32[4,4,4096]{2,1,0:T(4,128)} %param.36) | copy-start | bytes 786436
  57.4 70.1 %collective-permute-start.3 = (f32[3,384,128]{2,1,0:T(8,128)S(1)}, f32[3,384,128]{2,1,0:T(8,128)S(1)}, u32[]{:S(2)}, u32[]{:S(2)}) collective-permute-start(f32[3,384,128]{2,1,0:T(8,128)S(1)} %slice.26), channel_id=1, source_target_pairs={{8,0},{9,1},{10,2},{11,3},{12,4},{13,5},{14,6},{15,7},{0,8},{1,9},... | collective-permute-start | bytes 1769480 | tf_op jit(solution)/shard_map/cond/branch_3_fun/ppermute | solution.py:726
where the time goes:
time: 133 us
  waiting for transfers between devices  67.5 us (51%)
  Pallas kernels  52.2 us (39%)
  starting transfers between devices  5.7 us (4%)
  local copies, waits for them, and re-layouts  2.29 us (2%)
  matrix products  1.86 us (1%)
  other arithmetic  1.82 us (1%)
  between operations  1.49 us (1%)
    ppermute x1, waiting for transfers between devices, run(): got = lax.ppermute(cells[:count], 'cell', route)  67.4 us
    pallas_call x2, Pallas kernels, solve(): pl.pallas_call(functools.partial(solve_kernel, elems, points, begin, firs...  45 us
    pallas_call x1, Pallas kernels, local(): pl.pallas_call(functools.partial(merge_kernel, elems, points, first), out...  4.5 us
    pallas_call x1, Pallas kernels, local(): pl.pallas_call(functools.partial(pack_kernel, elems, points, first), out_...  2.69 us
  transfers between devices with their start and end apart: 5, of which 1 were waited for; matrix products, arithmetic and copies ran while one was open for 4% of the time, Pallas kernels for 0%

commit v1 on v0

--- a/solution.py
+++ b/solution.py
@@ -466,8 +466,8 @@
     points,
     first,
     order,
+    rem,
     s_head,
-    rem,
     got_p,
     got_s,
     shear,
@@ -481,41 +481,15 @@
     s_out,
     p_out,
     in_sem,
-    own_sem,
     out_sem,
 ):
     total = elems * points
     moving = order[total]
     rows = LINES * points
-    state_part = pl.ds(P_ROWS, S_ROWS)
-
-    def own_props(e_at):
-        return [
-            pltpu.make_async_copy(
-                source.at[pl.ds(pl.multiple_of(e_at * rows, 8), rows), :],
-                p_out.at[e_at, pl.ds(row * rows, rows), :],
-                own_sem.at[e_at],
-            )
-            for row, source in enumerate((shear, bulk, base, sat, rate))
-        ]
-
-    def arrival(cell, act):
-        slot = order[total + 1 + cell]
-        late = jnp.maximum(slot - first, 0)
-        sem = in_sem.at[cell]
-        moved, soon = slot < moving, slot < first
-
-        @pl.when(jnp.logical_not(moved) & soon)
-        def _():
-            act(
-                pltpu.make_async_copy(
-                    s_head.at[jnp.minimum(slot, first - 1)], cells.at[cell, state_part, :], sem
-                )
-            )
-
-        @pl.when(jnp.logical_not(soon))
-        def _():
-            act(pltpu.make_async_copy(rem.at[late], cells.at[cell], sem))
+
+    def arrival(slot):
+        late = slot - first
+        return pltpu.make_async_copy(rem.at[late], cells.at[late], in_sem.at[late])
 
     def leaving(e_at):
         return (
@@ -523,44 +497,52 @@
             pltpu.make_async_copy(p_out.at[e_at], new_props.at[e_at], out_sem.at[e_at, 1]),
         )
 
+    def put(target, cell, count, load):
+        for row in range(count):
+            for part in range(0, LINES, 8):
+                at = row * rows + part * points + cell % points
+                target[cell // points, pl.ds(at, 8, stride=points), :] = load(row * LINES + part)
+
+    @pl.loop(first, total)
+    def _(slot):
+        arrival(slot).start()
+
     @pl.loop(0, elems)
     def _(e_at):
-        for g_at in range(points):
-            arrival(e_at * points + g_at, lambda copy: copy.start())
-        for copy in own_props(e_at):
-            copy.start()
+        for row, source in enumerate((shear, bulk, base, sat, rate)):
+            p_out[e_at, pl.ds(row * rows, rows), :] = source[
+                pl.ds(pl.multiple_of(e_at * rows, rows), rows), :
+            ]
+
+    @pl.loop(0, first)
+    def _(slot):
+        cell = order[slot]
+
+        @pl.when(slot < moving)
+        def _():
+            put(p_out, cell, 5, lambda at: got_p[slot, at : at + 8, :])
+            put(s_out, cell, 7, lambda at: got_s[slot, at : at + 8, :])
+
+        @pl.when(slot >= moving)
+        def _():
+            put(s_out, cell, 7, lambda at: s_head[slot, at : at + 8, :])
 
     @pl.loop(0, elems)
     def _(e_at):
-        for copy in own_props(e_at):
-            copy.wait()
-
         @pl.loop(0, points)
         def _(g_at):
             cell = e_at * points + g_at
             slot = order[total + 1 + cell]
-            arrival(cell, lambda copy: copy.wait())
-            moved, soon = slot < moving, slot < first
-            early = jnp.minimum(slot, first - 1)
-
-            def put(target, count, load):
-                for row in range(count):
-                    for part in range(0, LINES, 8):
-                        at = row * rows + part * points + g_at
-                        target[e_at, pl.ds(at, 8, stride=points), :] = load(row * LINES + part)
-
-            @pl.when(moved & soon)
+            late = jnp.maximum(slot - first, 0)
+
+            @pl.when(slot >= first)
             def _():
-                put(p_out, 5, lambda at: got_p[early, at : at + 8, :])
-                put(s_out, 7, lambda at: got_s[early, at : at + 8, :])
-
-            @pl.when(moved & jnp.logical_not(soon))
+                arrival(jnp.maximum(slot, first)).wait()
+                put(s_out, cell, 7, lambda at: cells[late, P_ROWS + at : P_ROWS + at + 8, :])
+
+            @pl.when((slot >= first) & (slot < moving))
             def _():
-                put(p_out, 5, lambda at: cells[cell, at : at + 8, :])
-
-            @pl.when(jnp.logical_not(moved & soon))
-            def _():
-                put(s_out, 7, lambda at: cells[cell, P_ROWS + at : P_ROWS + at + 8, :])
+                put(p_out, cell, 5, lambda at: cells[late, at : at + 8, :])
 
         for copy in leaving(e_at):
             copy.start()
@@ -739,19 +721,18 @@
             shape(elems, 7 * LINES * points, LANES),
             shape(elems, 5 * LINES * points, LANES),
         ),
-        in_specs=[SMEM] + [ANY] * 2 + [VMEM] * 2 + [ANY] * 5,
+        in_specs=[SMEM, ANY] + [VMEM] * 8,
         out_specs=(ANY, ANY),
         scratch_shapes=[
-            pltpu.VMEM((total, ROWS, LANES), jnp.float32),
+            pltpu.VMEM((total - first, ROWS, LANES), jnp.float32),
             pltpu.VMEM((elems, 7 * LINES * points, LANES), jnp.float32),
             pltpu.VMEM((elems, 5 * LINES * points, LANES), jnp.float32),
-            pltpu.SemaphoreType.DMA((total,)),
-            pltpu.SemaphoreType.DMA((elems,)),
+            pltpu.SemaphoreType.DMA((total - first,)),
             pltpu.SemaphoreType.DMA((elems, 2)),
         ],
         compiler_params=pltpu.CompilerParams(vmem_limit_bytes=MERGE_GRANT),
         name="merge",
-    )(order, s_head, rem, got_p, got_s, *props)
+    )(order, rem, s_head, got_p, got_s, *props)
     return force, stiff, stress, whole(new_state, 7), whole(new_props, 5)
 
 

time: 133 us -> 132 us (level)
  no operation moved by 1% of the time
where the time goes in v1:
time: 132 us
  waiting for transfers between devices  67.5 us (51%)
  Pallas kernels  51.4 us (39%)
  starting transfers between devices  5.7 us (4%)
  local copies, waits for them, and re-layouts  2.29 us (2%)
  matrix products  1.86 us (1%)
  other arithmetic  1.82 us (1%)
  between operations  1.49 us (1%)
    ppermute x1, waiting for transfers between devices, run(): got = lax.ppermute(cells[:count], 'cell', route)  67.4 us
    pallas_call x2, Pallas kernels, solve(): pl.pallas_call(functools.partial(solve_kernel, elems, points, begin, firs...  45 us
    pallas_call x1, Pallas kernels, local(): pl.pallas_call(functools.partial(merge_kernel, elems, points, first), out...  3.7 us
    pallas_call x1, Pallas kernels, local(): pl.pallas_call(functools.partial(pack_kernel, elems, points, first), out_...  2.69 us
    ppermute x1, starting transfers between devices, run(): got = lax.ppermute(cells[:count], 'cell', route)  2.66 us
  transfers between devices with their start and end apart: 5, of which 1 were waited for; matrix products, arithmetic and copies ran while one was open for 4% of the time, Pallas kernels for 0%

profile of v1, /device:TPU:2, one launch (start us, length us, event | category | flops | bytes accessed | tf_op | source)
XLA Modules:
  0.0 132.1 jit_solution(4931423781758431826)
XLA Ops:
  0.6 2.7 %pack.1 = (s32[33]{0:T(128)}, f32[6,160,128]{2,1,0:T(8,128)}) custom-call(s32[4,4]{1,0:T(4,128)} %flag.1, f32[512,128]{1,0:T(8,128)} %bitcast.69, f32[512,128]{1,0:T(8,128)} %bitcast.73, f32[512,128]{1,0:T(8,128)} %bitcast.77, f32[512,128]{1,0:T(8,128)} %bitcast.81, f32[512,128]{1,0:T(8,128)} %bitcast.85), custom_call_target="tpu_custom_call" | custom-call | tf_op jit(solution)/shard_map/pack/pallas_call | solution.py:632
  3.3 22.1 %solve.2 = (f32[6,224,128]{2,1,0:T(8,128)}, f32[2,384,128]{2,1,0:T(8,128)}, f32[8,128]{1,0:T(8,128)}) custom-call(s32[33]{0:T(128)} %get-tuple-element.41.order, s32[4,4]{1,0:T(4,128)} %fft_iters.3, s32[4,4]{1,0:T(4,128)} %rm_iters.3, f32[4,1,24]{2,1,0:T(1,128)} %bitcast.98, f32[8,6,24]{2,1,0:T(8,128)} %constant.55.clone.bmat, f32[3072,128]{1,0:T(8,128)} %bitcast.93, ...), custom_call_target="tpu_custom_call" | custom-call | flops 20000000000 | bytes 8000000 | tf_op jit(solution)/shard_map/solve/pallas_call | solution.py:651
  25.5 0.0 copy-start.6
  25.5 0.0 copy-start.11
  25.5 0.0 copy-start.12
  25.5 0.0 copy-start.8
  25.5 0.0 copy-start.5
  25.5 0.0 copy-start.9
  25.5 0.0 copy-start.10
  25.6 22.9 %solve.3 = (f32[10,384,128]{2,1,0:T(8,128)}, f32[8,128]{1,0:T(8,128)}) custom-call(s32[33]{0:T(128)} %get-tuple-element.41.order, s32[4,4]{1,0:T(4,128)} %fft_iters.3, s32[4,4]{1,0:T(4,128)} %rm_iters.3, f32[4,1,24]{2,1,0:T(1,128)} %bitcast.99, f32[8,6,24]{2,1,0:T(8,128)} %constant.55.clone.bmat, f32[3072,128]{1,0:T(8,128)} %bitcast.94, ...), custom_call_target="tpu_custom_call" | custom-call | flops 20000000000 | bytes 8000000 | tf_op jit(solution)/shard_map/solve/pallas_call | solution.py:651
  48.4 0.0 copy-done.6
  48.4 0.0 copy-done.11
  48.5 0.8 fusion.7
  49.3 0.0 copy-done.12
  49.3 0.0 copy-done.8
  49.3 0.2 fusion.1
  49.5 0.0 collective-permute-start.10
  49.5 2.6 %collective-permute-start.12 = (f32[6,160,128]{2,1,0:T(8,128)}, f32[6,160,128]{2,1,0:T(8,128)S(1)}, u32[]{:S(2)}, u32[]{:S(2)}) collective-permute-start(f32[6,160,128]{2,1,0:T(8,128)} %get-tuple-element.51), channel_id=1, source_target_pairs={{8,0},{9,1},{10,2},{11,3},{12,4},{13,5},{14,6},{15,7},{0,8},{1,9},... | collective-permute-start | bytes 1474568 | tf_op jit(solution)/shard_map/ppermute | solution.py:641
  52.1 0.0 copy-done.5
  52.1 0.3 collective-permute-start.13
  52.5 0.0 copy-done.9
  52.5 0.2 fusion.5
  52.7 0.1 reshape.94
  52.8 0.4 convolution_bitcast_fusion
  53.1 0.3 fusion
  53.4 0.1 div.18
  53.5 0.1 collective-permute-start.11
  53.6 0.0 copy-done.10
  53.6 0.6 convert_reduce_fusion
  54.9 0.0 collective-permute-done.10
  54.9 0.6 add.11
  55.5 0.0 collective-permute-done.11
  55.5 0.6 add.12
  56.1 0.0 copy-start.4
  56.1 0.0 copy-done.7
  56.1 72.2 %conditional.1 = (f32[10,384,128]{2,1,0:T(8,128)}) conditional(s32[]{:T(128)} %clamp.3, f32[10,384,128]{2,1,0:T(8,128)} %get-tuple-element.49, f32[10,384,128]{2,1,0:T(8,128)} %get-tuple-element.49, f32[10,384,128]{2,1,0:T(8,128)} %get-tuple-element.49, f32[10,384,128]{2,1,0:T(8,128)} %get-tuple-element.49, ...), branch_computations={%region_1.2_spmd, %region_2.3_spmd, %region_3.4_spmd, %region_4.5_... | conditional | bytes 14155824 | solution.py:716
  56.2 1.2 slice.26
  57.4 2.7 %collective-permute-start.3 = (f32[3,384,128]{2,1,0:T(8,128)S(1)}, f32[3,384,128]{2,1,0:T(8,128)S(1)}, u32[]{:S(2)}, u32[]{:S(2)}) collective-permute-start(f32[3,384,128]{2,1,0:T(8,128)S(1)} %slice.26), channel_id=1, source_target_pairs={{8,0},{9,1},{10,2},{11,3},{12,4},{13,5},{14,6},{15,7},{0,8},{1,9},... | collective-permute-start | bytes 1769480 | tf_op jit(solution)/shard_map/cond/branch_3_fun/ppermute | solution.py:708
  60.0 67.4 %collective-permute-done.3 = f32[3,384,128]{2,1,0:T(8,128)S(1)} collective-permute-done((f32[3,384,128]{2,1,0:T(8,128)S(1)}, f32[3,384,128]{2,1,0:T(8,128)S(1)}, u32[]{:S(2)}, u32[]{:S(2)}) %collective-permute-start.3) | collective-permute-done | bytes 589856 | tf_op jit(solution)/shard_map/cond/branch_3_fun/ppermute | solution.py:708
  127.5 0.9 constant_dynamic-update-slice_fusion.2
  128.3 0.0 collective-permute-done.12.got_p
  128.3 0.0 collective-permute-done.13.got_s
  128.3 0.0 copy-done
  128.3 0.0 copy-done.1
  128.3 0.0 copy-done.2
  128.4 0.0 copy-done.3
  128.4 0.0 copy-done.4
  128.4 3.7 %merge.1 = (f32[4,896,128]{2,1,0:T(8,128)}, f32[4,640,128]{2,1,0:T(8,128)}) custom-call(s32[33]{0:T(128)S(1)} %copy-done.6, f32[10,384,128]{2,1,0:T(8,128)} %get-tuple-element.54.rem, f32[6,224,128]{2,1,0:T(8,128)S(1)} %copy-done.5, f32[6,160,128]{2,1,0:T(8,128)S(1)} %collective-permute-done.12.got_p, f32[6,224,128]{2,1,0:T(8,128)S(1)} %collective-permute-done.13.got_s, ...), custom_call_target="tpu_custom_call" | custom-call | tf_op jit(solution)/shard_map/merge/pallas_call | solution.py:718
  (6 shorter events, 0.0 us)
Async XLA Ops:
  25.5 23.0 %copy-start.6 = (s32[33]{0:T(128)S(1)}, s32[33]{0:T(128)}, u32[]{:S(2)}) copy-start(s32[33]{0:T(128)} %get-tuple-element.41.order) | copy-start | bytes 400
  25.5 23.0 %copy-start.11 = (f32[8,128]{1,0:T(8,128)S(1)}, f32[8,128]{1,0:T(8,128)}, u32[]{:S(2)}) copy-start(f32[8,128]{1,0:T(8,128)} %get-tuple-element.44) | copy-start | bytes 12292
  25.5 23.8 %copy-start.12 = (f32[6]{0:T(128)S(1)}, f32[6]{0:T(128)}, u32[]{:S(2)}) copy-start(f32[6]{0:T(128)} %constant.60.clone) | copy-start | bytes 76
  25.5 23.8 %copy-start.8 = (f32[8,6,24]{2,1,0:T(8,128)S(1)}, f32[8,6,24]{2,1,0:T(8,128)}, u32[]{:S(2)}) copy-start(f32[8,6,24]{2,1,0:T(8,128)} %constant.55.clone.bmat) | copy-start | bytes 13828
  25.5 26.6 %copy-start.5 = (f32[6,224,128]{2,1,0:T(8,128)S(1)}, f32[6,224,128]{2,1,0:T(8,128)}, u32[]{:S(2)}) copy-start(f32[6,224,128]{2,1,0:T(8,128)} %get-tuple-element.50.s_head) | copy-start | bytes 2064388
  25.5 27.0 %copy-start.9 = (f32[23,36]{1,0:T(8,128)S(1)}, f32[23,36]{1,0:T(8,128)}, u32[]{:S(2)}) copy-start(f32[23,36]{1,0:T(8,128)} %constant.59.clone) | copy-start | bytes 9940
  25.5 28.1 %copy-start.10 = (s32[4,4]{1,0:T(4,128)S(1)}, s32[4,4]{1,0:T(4,128)}, u32[]{:S(2)}) copy-start(s32[4,4]{1,0:T(4,128)} %flag.1) | copy-start | bytes 196
  49.3 6.9 %copy-start.7 = (f32[16,128]{1,0:T(8,128)}, f32[16,128]{1,0:T(8,128)S(1)}, u32[]{:S(2)}) copy-start(f32[16,128]{1,0:T(8,128)S(1)} %fusion.7) | copy-start | bytes 24580
  49.5 5.4 %collective-permute-start.10 = (f32[4,24]{1,0:T(4,128)S(1)}, f32[4,24]{1,0:T(4,128)S(1)}, u32[]{:S(2)}, u32[]{:S(2)}) collective-permute-start(f32[4,24]{1,0:T(4,128)S(1)} %fusion.1), channel_id=1, source_target_pairs={{16,0},{0,16},{17,1},{1,17},{18,2},{2,18},{19,3},{3,19},{20,4},{4,... | collective-permute-start | bytes 1160 | tf_op jit(solution)/shard_map/ppermute | solution.py:700
  49.5 78.8 %collective-permute-start.12 = (f32[6,160,128]{2,1,0:T(8,128)}, f32[6,160,128]{2,1,0:T(8,128)S(1)}, u32[]{:S(2)}, u32[]{:S(2)}) collective-permute-start(f32[6,160,128]{2,1,0:T(8,128)} %get-tuple-element.51), channel_id=1, source_target_pairs={{8,0},{9,1},{10,2},{11,3},{12,4},{13,5},{14,6},{15,7},{0,8},{1,9},... | collective-permute-start | bytes 1474568 | tf_op jit(solution)/shard_map/ppermute | solution.py:641
  52.1 76.2 %collective-permute-start.13 = (f32[6,224,128]{2,1,0:T(8,128)S(1)}, f32[6,224,128]{2,1,0:T(8,128)S(1)}, u32[]{:S(2)}, u32[]{:S(2)}) collective-permute-start(f32[6,224,128]{2,1,0:T(8,128)S(1)} %copy-done.5), channel_id=1, source_target_pairs={{8,0},{9,1},{10,2},{11,3},{12,4},{13,5},{14,6},{15,7},{0,8},{1,9},... | collective-permute-start | bytes 2064392 | tf_op jit(solution)/shard_map/ppermute | solution.py:686
  53.5 2.0 %collective-permute-start.11 = (f32[4,576]{1,0:T(4,128)S(1)}, f32[4,576]{1,0:T(4,128)S(1)}, u32[]{:S(2)}, u32[]{:S(2)}) collective-permute-start(f32[4,576]{1,0:T(4,128)S(1)} %div.18), channel_id=1, source_target_pairs={{16,0},{0,16},{17,1},{1,17},{18,2},{2,18},{19,3},{3,19},{20,4},{4,... | collective-permute-start | bytes 27656 | tf_op jit(solution)/shard_map/ppermute | solution.py:701
  56.1 72.2 %copy-start = (f32[4,4,4096]{2,1,0:T(4,128)S(1)}, f32[4,4,4096]{2,1,0:T(4,128)}, u32[]{:S(2)}) copy-start(f32[4,4,4096]{2,1,0:T(4,128)} %param.32) | copy-start | bytes 786436
  56.1 72.3 %copy-start.1 = (f32[4,4,4096]{2,1,0:T(4,128)S(1)}, f32[4,4,4096]{2,1,0:T(4,128)}, u32[]{:S(2)}) copy-start(f32[4,4,4096]{2,1,0:T(4,128)} %param.33) | copy-start | bytes 786436
  56.1 72.3 %copy-start.2 = (f32[4,4,4096]{2,1,0:T(4,128)S(1)}, f32[4,4,4096]{2,1,0:T(4,128)}, u32[]{:S(2)}) copy-start(f32[4,4,4096]{2,1,0:T(4,128)} %param.34) | copy-start | bytes 786436
  56.1 72.3 %copy-start.3 = (f32[4,4,4096]{2,1,0:T(4,128)S(1)}, f32[4,4,4096]{2,1,0:T(4,128)}, u32[]{:S(2)}) copy-start(f32[4,4,4096]{2,1,0:T(4,128)} %param.35) | copy-start | bytes 786436
  56.1 72.3 %copy-start.4 = (f32[4,4,4096]{2,1,0:T(4,128)S(1)}, f32[4,4,4096]{2,1,0:T(4,128)}, u32[]{:S(2)}) copy-start(f32[4,4,4096]{2,1,0:T(4,128)} %param.36) | copy-start | bytes 786436
  57.4 70.1 %collective-permute-start.3 = (f32[3,384,128]{2,1,0:T(8,128)S(1)}, f32[3,384,128]{2,1,0:T(8,128)S(1)}, u32[]{:S(2)}, u32[]{:S(2)}) collective-permute-start(f32[3,384,128]{2,1,0:T(8,128)S(1)} %slice.26), channel_id=1, source_target_pairs={{8,0},{9,1},{10,2},{11,3},{12,4},{13,5},{14,6},{15,7},{0,8},{1,9},... | collective-permute-start | bytes 1769480 | tf_op jit(solution)/shard_map/cond/branch_3_fun/ppermute | solution.py:708

commit v2 on v1

--- a/solution.py
+++ b/solution.py
@@ -6,6 +6,7 @@
 import numpy as np
 from jax import lax
 from jax.experimental import pallas as pl
+from jax.experimental.layout import Layout, with_layout_constraint
 from jax.experimental.pallas import tpu as pltpu
 from jax.sharding import PartitionSpec as P
 
@@ -18,6 +19,7 @@
 SLOPE = 0.05
 top_precision = lax.Precision.HIGHEST
 SUMS = 29
+PAIRS = 2
 LINES = GRID * PLANE // LANES
 P_ROWS = 5 * LINES
 S_ROWS = 7 * LINES
@@ -155,8 +157,7 @@
     field,
     work,
     spec,
-    part_hi,
-    part_lo,
+    parts,
     acc,
 ):
     total = elems * points
@@ -276,7 +277,19 @@
         inc = jnp.where(second, newton(over, inc, mu3, rest, rate), inc)
         return jnp.where(third, newton(over, inc, mu3, rest, rate), inc)
 
-    def stress_step(pair, carry):
+    def split_rows(comp):
+        if comp < 3:
+            return comp * block, (3 + comp) * block
+        return 2 * comp * block, (2 * comp + 1) * block
+
+    def split_store(comp, pair, half, value):
+        upper = value.astype(jnp.bfloat16)
+        lower = (value - upper.astype(jnp.float32)).astype(jnp.bfloat16)
+        lanes = slice(half * LANES, (half + 1) * LANES)
+        for base, part in zip(split_rows(comp), (upper, lower)):
+            parts[pl.ds(base + pair * 16, 16), lanes] = part
+
+    def stress_pair(pair):
         for half in range(2):
             load, volume, mu, dev, squared = trial(half, pair)
             base = load(9)
@@ -290,42 +303,37 @@
                 value = shrink * dev[comp]
                 if comp < 3:
                     value = value + pressure
-                upper = value.astype(jnp.bfloat16)
-                at = pl.ds(comp * block + pair * 16, 16)
-                lanes = slice(half * LANES, (half + 1) * LANES)
-                part_hi[at, lanes] = upper
-                part_lo[at, lanes] = (value - upper.astype(jnp.float32)).astype(jnp.bfloat16)
+                split_store(comp, pair, half, value)
+
+    def stress_step(step, carry):
+        for near in range(PAIRS):
+            stress_pair(step * PAIRS + near)
         return carry
 
     def plane_product(store):
-        for which, (from_row, rows) in enumerate(
-            ((0, 3 * block), (3 * block, block), (4 * block, block), (5 * block, block))
-        ):
-            for at in range(from_row, from_row + rows, block):
-                left_hi = part_hi[at : at + block, :]
-                left_lo = part_lo[at : at + block, :]
-                dot = functools.partial(jnp.dot, preferred_element_type=jnp.float32)
-                store(
-                    at,
-                    dot(left_hi, high[which])
-                    + (dot(left_lo, high[which]) + dot(left_hi, low[which])),
-                )
+        dot = functools.partial(jnp.dot, preferred_element_type=jnp.float32)
+        for which, comps in enumerate(((0, 1, 2), (3,), (4,), (5,))):
+            from_row, rows = split_rows(comps[0])[0], len(comps) * block
+            both = dot(parts[from_row : from_row + 2 * rows, :], high[which])
+            rest = dot(parts[from_row : from_row + rows, :], low[which])
+            store(comps[0] * block, both[:rows] + (both[rows:] + rest))
 
     def store_spec(at, value):
         for half in range(2):
-            work[half, at : at + block, :] = value[:, half * LANES : (half + 1) * LANES]
+            work[half, at : at + value.shape[0], :] = value[:, half * LANES : (half + 1) * LANES]
 
     def update_field(at, value):
         for half in range(2):
-            field[half, at : at + block, :] = (
-                field[half, at : at + block, :] - value[:, half * LANES : (half + 1) * LANES]
+            field[half, at : at + value.shape[0], :] = (
+                field[half, at : at + value.shape[0], :]
+                - value[:, half * LANES : (half + 1) * LANES]
             )
 
     def flip(comp, k):
         return (-k) % GRID if comp in (4, 5) else k
 
     def sweep(index, carry):
-        lax.fori_loop(0, GRID // 2, stress_step, 0)
+        lax.fori_loop(0, GRID // (2 * PAIRS), stress_step, 0)
         plane_product(store_spec)
         scale_cell = jnp.where(index < fft_count, inv_mu, 0.0)
 
@@ -383,13 +391,7 @@
                 )
                 for pair in range(GRID // 2):
                     value = jnp.concatenate([lines[2 * pair], lines[2 * pair + 1]], axis=0)
-                    upper = value.astype(jnp.bfloat16)
-                    at = comp * block + pair * 16
-                    lanes = slice(half * LANES, (half + 1) * LANES)
-                    part_hi[at : at + 16, lanes] = upper
-                    part_lo[at : at + 16, lanes] = (value - upper.astype(jnp.float32)).astype(
-                        jnp.bfloat16
-                    )
+                    split_store(comp, pair, half, value)
         plane_product(update_field)
         return carry
 
@@ -461,7 +463,14 @@
                         ]
 
 
-def merge_kernel(
+def put_cell(target, cell, points, count, load):
+    for row in range(count):
+        for part in range(0, LINES, 8):
+            at = (row * LINES + part) * points + cell % points
+            target[cell // points, pl.ds(at, 8, stride=points), :] = load(row * LINES + part)
+
+
+def gather_kernel(
     elems,
     points,
     first,
@@ -475,13 +484,10 @@
     base,
     sat,
     rate,
-    new_state,
-    new_props,
-    cells,
     s_out,
     p_out,
+    cells,
     in_sem,
-    out_sem,
 ):
     total = elems * points
     moving = order[total]
@@ -491,19 +497,9 @@
         late = slot - first
         return pltpu.make_async_copy(rem.at[late], cells.at[late], in_sem.at[late])
 
-    def leaving(e_at):
-        return (
-            pltpu.make_async_copy(s_out.at[e_at], new_state.at[e_at], out_sem.at[e_at, 0]),
-            pltpu.make_async_copy(p_out.at[e_at], new_props.at[e_at], out_sem.at[e_at, 1]),
-        )
-
-    def put(target, cell, count, load):
-        for row in range(count):
-            for part in range(0, LINES, 8):
-                at = row * rows + part * points + cell % points
-                target[cell // points, pl.ds(at, 8, stride=points), :] = load(row * LINES + part)
-
-    @pl.loop(first, total)
+    from_slot = jnp.maximum(moving, first)
+
+    @pl.loop(from_slot, total)
     def _(slot):
         arrival(slot).start()
 
@@ -520,29 +516,61 @@
 
         @pl.when(slot < moving)
         def _():
-            put(p_out, cell, 5, lambda at: got_p[slot, at : at + 8, :])
-            put(s_out, cell, 7, lambda at: got_s[slot, at : at + 8, :])
+            put_cell(p_out, cell, points, 5, lambda at: got_p[slot, at : at + 8, :])
+            put_cell(s_out, cell, points, 7, lambda at: got_s[slot, at : at + 8, :])
 
         @pl.when(slot >= moving)
         def _():
-            put(s_out, cell, 7, lambda at: s_head[slot, at : at + 8, :])
+            put_cell(s_out, cell, points, 7, lambda at: s_head[slot, at : at + 8, :])
+
+    @pl.loop(from_slot, total)
+    def _(slot):
+        late = slot - first
+        arrival(slot).wait()
+        put_cell(
+            s_out,
+            order[slot],
+            points,
+            7,
+            lambda at: cells[late, P_ROWS + at : P_ROWS + at + 8, :],
+        )
+
+
+def finish_kernel(
+    elems, points, first, count, order, near_s, near_p, *refs
+):
+    got = refs[0] if count else None
+    new_state, new_props, s_out, p_out, out_sem = refs[1 if count else 0 :]
+    total = elems * points
+
+    def leaving(e_at):
+        return (
+            pltpu.make_async_copy(s_out.at[e_at], new_state.at[e_at], out_sem.at[e_at, 0]),
+            pltpu.make_async_copy(p_out.at[e_at], new_props.at[e_at], out_sem.at[e_at, 1]),
+        )
 
     @pl.loop(0, elems)
     def _(e_at):
-        @pl.loop(0, points)
-        def _(g_at):
-            cell = e_at * points + g_at
-            slot = order[total + 1 + cell]
-            late = jnp.maximum(slot - first, 0)
-
-            @pl.when(slot >= first)
-            def _():
-                arrival(jnp.maximum(slot, first)).wait()
-                put(s_out, cell, 7, lambda at: cells[late, P_ROWS + at : P_ROWS + at + 8, :])
-
-            @pl.when((slot >= first) & (slot < moving))
-            def _():
-                put(p_out, cell, 5, lambda at: cells[late, at : at + 8, :])
+        s_out[e_at] = near_s[e_at]
+        p_out[e_at] = near_p[e_at]
+        if count:
+
+            @pl.loop(0, points)
+            def _(g_at):
+                cell = e_at * points + g_at
+                slot = order[total + 1 + cell]
+                late = jnp.clip(slot - first, 0, count - 1)
+
+                @pl.when((slot >= first) & (slot < first + count))
+                def _():
+                    put_cell(p_out, cell, points, 5, lambda at: got[late, at : at + 8, :])
+                    put_cell(
+                        s_out,
+                        cell,
+                        points,
+                        7,
+                        lambda at: got[late, P_ROWS + at : P_ROWS + at + 8, :],
+                    )
 
         for copy in leaving(e_at):
             copy.start()
@@ -625,7 +653,8 @@
 
     def whole(lines, lead):
         tiles = lines.reshape(elems, lead, LINES, points, LANES)
-        return jnp.moveaxis(tiles, 3, 1).reshape(elems, points, lead, voxels)
+        tiles = with_layout_constraint(jnp.moveaxis(tiles, 3, 1), Layout((0, 2, 3, 1, 4)))
+        return tiles.reshape(elems, points, lead, voxels)
 
     props = [flat(a) for a in (shear_mod, bulk_mod, yield_stress, sat_stress, sat_rate)]
     hard, plastic = flat(hardening_var), flat(plastic_strain)
@@ -658,8 +687,7 @@
                 pltpu.VMEM((2, 6 * block, LANES), jnp.float32),
                 pltpu.VMEM((2, 6 * block, LANES), jnp.float32),
                 pltpu.VMEM((2, 6 * block, LANES), jnp.float32),
-                pltpu.VMEM((6 * block, PLANE), jnp.bfloat16),
-                pltpu.VMEM((6 * block, PLANE), jnp.bfloat16),
+                pltpu.VMEM((2 * 6 * block, PLANE), jnp.bfloat16),
                 pltpu.VMEM((SUMS, BATCH, LANES), jnp.float32),
             ],
             compiler_params=params,
@@ -701,38 +729,61 @@
         stiff = stiff + lax.ppermute(stiff_part, "sec", ring)
     rem, force, stiff, stress = lax.optimization_barrier((rem, force, stiff, stress))
 
+    blocks = (
+        shape(elems, 7 * LINES * points, LANES),
+        shape(elems, 5 * LINES * points, LANES),
+    )
+    ends = pltpu.CompilerParams(vmem_limit_bytes=MERGE_GRANT)
+
     def branch(count):
-        def run(cells):
-            if count == 0:
-                return cells
-            got = lax.ppermute(cells[:count], "cell", route)
-            return lax.dynamic_update_slice_in_dim(cells, got, 0, 0)
+        def run(order, rem, s_head, got_p, got_s, *props):
+            late = ()
+            if count:
+                late = (lax.ppermute(rem[:count], "cell", route),)
+            near = pl.pallas_call(
+                functools.partial(gather_kernel, elems, points, first),
+                out_shape=blocks,
+                in_specs=[SMEM, ANY] + [VMEM] * 8,
+                out_specs=(VMEM, VMEM),
+                scratch_shapes=[
+                    pltpu.VMEM((total - first, ROWS, LANES), jnp.float32),
+                    pltpu.SemaphoreType.DMA((total - first,)),
+                ],
+                compiler_params=ends,
+                cost_estimate=pl.CostEstimate(
+                    flops=10**9, bytes_accessed=6 * 10**6, transcendentals=0
+                ),
+                name="gather",
+            )(order, rem, s_head, got_p, got_s, *props)
+            new_state, new_props = pl.pallas_call(
+                functools.partial(finish_kernel, elems, points, first, count),
+                out_shape=blocks,
+                in_specs=[SMEM] + [VMEM] * (2 + len(late)),
+                out_specs=(ANY, ANY),
+                scratch_shapes=[
+                    *[pltpu.VMEM(block.shape, jnp.float32) for block in blocks],
+                    pltpu.SemaphoreType.DMA((elems, 2)),
+                ],
+                compiler_params=ends,
+                name="finish",
+            )(order, *near, *late)
+            return new_state, new_props
 
         return run
 
     extra = jnp.clip(
         jnp.sum((move_flag > 0).astype(jnp.int32)) - first, 0, total - first
     )
-    rem = lax.switch(extra, [branch(c) for c in range(total - first + 1)], rem)
-
-    new_state, new_props = pl.pallas_call(
-        functools.partial(merge_kernel, elems, points, first),
-        out_shape=(
-            shape(elems, 7 * LINES * points, LANES),
-            shape(elems, 5 * LINES * points, LANES),
-        ),
-        in_specs=[SMEM, ANY] + [VMEM] * 8,
-        out_specs=(ANY, ANY),
-        scratch_shapes=[
-            pltpu.VMEM((total - first, ROWS, LANES), jnp.float32),
-            pltpu.VMEM((elems, 7 * LINES * points, LANES), jnp.float32),
-            pltpu.VMEM((elems, 5 * LINES * points, LANES), jnp.float32),
-            pltpu.SemaphoreType.DMA((total - first,)),
-            pltpu.SemaphoreType.DMA((elems, 2)),
-        ],
-        compiler_params=pltpu.CompilerParams(vmem_limit_bytes=MERGE_GRANT),
-        name="merge",
-    )(order, rem, s_head, got_p, got_s, *props)
+    new_state, new_props = lax.switch(
+        extra,
+        [branch(c) for c in range(total - first + 1)],
+        order,
+        rem,
+        s_head,
+        got_p,
+        got_s,
+        *props,
+    )
     return force, stiff, stress, whole(new_state, 7), whole(new_props, 5)
 
 

time: 132 us -> 83.6 us (0.63)
  waiting for transfers between devices: 67.5 us -> 22.9 us
  starting transfers between devices: 5.7 us -> 3.63 us
  local copies, waits for them, and re-layouts: 2.29 us -> 0.23 us
    ppermute x1, waiting for transfers between devices: 67.4 us -> 19.5 us  [run(): late = (lax.ppermute(rem[:count], 'cell', route),)]
    ppermute x1, waiting for transfers between devices: 0.01 us -> 3.39 us  [local(): got_s = lax.ppermute(s_head, 'cell', route)]
    ppermute x1, starting transfers between devices: 2.66 us -> 0.07 us  [run(): late = (lax.ppermute(rem[:count], 'cell', route),)]
    pallas_call x1 -> x2, Pallas kernels: 3.7 us -> 6.18 us  [the longest x1 3.8 us: run(): pl.pallas_call(functools.partial(gather_kernel, elems, points, first), ou...]
    pallas_call x2, Pallas kernels: 45 us -> 42.6 us  [solve(): pl.pallas_call(functools.partial(solve_kernel, elems, points, begin, firs...]
  transfers between devices with their start and end apart: 5 -> 5, of which waited for: 1 -> 2; matrix products, arithmetic and copies ran while one was open for 4% -> 5% of each run, Pallas kernels for 0% -> 56%
where the time goes in v2:
time: 83.6 us; the launch traced here: 83.4 us
  Pallas kernels  51.5 us (62%)
  waiting for transfers between devices  22.9 us (27%)
  starting transfers between devices  3.63 us (4%)
  matrix products  1.86 us (2%)
  other arithmetic  1.82 us (2%)
  between operations  1.37 us (2%)
    pallas_call x2, Pallas kernels, solve(): pl.pallas_call(functools.partial(solve_kernel, elems, points, begin, firs...  42.6 us
    ppermute x1, waiting for transfers between devices, run(): late = (lax.ppermute(rem[:count], 'cell', route),)  19.5 us
    pallas_call x1, Pallas kernels, run(): pl.pallas_call(functools.partial(gather_kernel, elems, points, first), ou...  3.8 us
    ppermute x1, waiting for transfers between devices, local(): got_s = lax.ppermute(s_head, 'cell', route)  3.39 us
    pallas_call x1, Pallas kernels, local(): pl.pallas_call(functools.partial(pack_kernel, elems, points, first), out_...  2.69 us
    ppermute x1, starting transfers between devices, local(): got_p = lax.ppermute(p_head, 'cell', route)  2.65 us
    pallas_call x1, Pallas kernels, run(): pl.pallas_call(functools.partial(finish_kernel, elems, points, first, cou...  2.38 us
  transfers between devices with their start and end apart: 5, of which 2 were waited for; matrix products, arithmetic and copies ran while one was open for 5% of the time, Pallas kernels for 56%

profile of v2, /device:TPU:2, one launch (start us, length us, event | category | flops | bytes accessed | tf_op | source)
XLA Modules:
  0.0 83.4 jit_solution(7843442797139081798)
XLA Ops:
  0.6 2.7 %pack.1 = (s32[33]{0:T(128)S(1)}, f32[6,160,128]{2,1,0:T(8,128)}) custom-call(s32[4,4]{1,0:T(4,128)} %flag.1, f32[512,128]{1,0:T(8,128)} %bitcast.69, f32[512,128]{1,0:T(8,128)} %bitcast.83, f32[512,128]{1,0:T(8,128)} %bitcast.97, f32[512,128]{1,0:T(8,128)} %bitcast.111, f32[512,128]{1,0:T(8,128)} %bitcast.125), custom_call_target="tpu_custom_call" | custom-call | tf_op jit(solution)/shard_map/pack/pallas_call | solution.py:661
  3.3 2.7 %collective-permute-start.12 = (f32[6,160,128]{2,1,0:T(8,128)}, f32[6,160,128]{2,1,0:T(8,128)}, u32[]{:S(2)}, u32[]{:S(2)}) collective-permute-start(f32[6,160,128]{2,1,0:T(8,128)} %get-tuple-element.380), channel_id=1, source_target_pairs={{8,0},{9,1},{10,2},{11,3},{12,4},{13,5},{14,6},{15,7},{0,8},{1,9},... | collective-permute-start | bytes 1474568 | tf_op jit(solution)/shard_map/ppermute | solution.py:670
  6.0 21.4 %solve.2 = (f32[6,224,128]{2,1,0:T(8,128)S(1)}, f32[2,384,128]{2,1,0:T(8,128)}, f32[8,128]{1,0:T(8,128)}) custom-call(s32[33]{0:T(128)S(1)} %get-tuple-element.370.order, s32[4,4]{1,0:T(4,128)} %fft_iters.3, s32[4,4]{1,0:T(4,128)} %rm_iters.3, f32[4,1,24]{2,1,0:T(1,128)} %bitcast.148, f32[8,6,24]{2,1,0:T(8,128)} %constant.37.clone.bmat, ...), custom_call_target="tpu_custom_call" | custom-call | flops 20000000000 | bytes 8000000 | tf_op jit(solution)/shard_map/solve/pallas_call | solution.py:680
  27.3 0.3 collective-permute-start.13
  27.7 0.0 copy-start.34
  27.7 0.0 copy-start.35
  27.7 0.0 copy-start.31
  27.7 0.0 copy-start.32
  27.7 0.0 copy-start.33
  27.7 21.2 %solve.3 = (f32[10,384,128]{2,1,0:T(8,128)S(1)}, f32[8,128]{1,0:T(8,128)}) custom-call(s32[33]{0:T(128)S(1)} %get-tuple-element.370.order, s32[4,4]{1,0:T(4,128)} %fft_iters.3, s32[4,4]{1,0:T(4,128)} %rm_iters.3, f32[4,1,24]{2,1,0:T(1,128)} %bitcast.149, f32[8,6,24]{2,1,0:T(8,128)} %constant.37.clone.bmat, f32[3072,128]{1,0:T(8,128)} %bitcast.144, ...), custom_call_target="tpu_custom_call" | custom-call | flops 20000000000 | bytes 8000000 | tf_op jit(solution)/shard_map/solve/pallas_call | solution.py:680
  48.9 0.0 copy-done.34
  48.9 0.8 fusion.7
  49.8 0.0 copy-start.30
  49.8 0.0 copy-done.35
  49.8 0.0 copy-done.31
  49.8 0.2 fusion.1
  50.0 0.0 collective-permute-start.10
  50.0 0.0 copy-done.32
  50.0 0.2 fusion.5
  50.2 0.1 reshape.94
  50.3 0.4 convolution_bitcast_fusion
  50.7 0.3 fusion
  50.9 0.1 div.18
  51.0 0.6 collective-permute-start.11
  51.6 0.0 copy-done.33
  51.6 0.6 convert_reduce_fusion
  52.9 0.0 collective-permute-done.10
  52.9 0.6 add.11
  53.5 0.0 collective-permute-done.11
  53.5 0.6 add.12
  54.1 0.0 collective-permute-done.12
  54.1 3.4 %collective-permute-done.13 = f32[6,224,128]{2,1,0:T(8,128)S(1)} collective-permute-done((f32[6,224,128]{2,1,0:T(8,128)S(1)}, f32[6,224,128]{2,1,0:T(8,128)S(1)}, u32[]{:S(2)}, u32[]{:S(2)}) %collective-permute-start.13) | collective-permute-done | bytes 688160 | tf_op jit(solution)/shard_map/ppermute | solution.py:714
  57.5 0.0 copy-done.30
  57.5 25.9 %conditional.1 = ((f32[4,896,128]{2,1,0:T(8,128)}, f32[4,640,128]{2,1,0:T(8,128)})) conditional(s32[]{:T(128)} %clamp.3, (s32[33]{0:T(128)S(1)}, f32[10,384,128]{2,1,0:T(8,128)S(1)}, f32[6,224,128]{2,1,0:T(8,128)S(1)}, f32[6,160,128]{2,1,0:T(8,128)}, f32[6,224,128]{2,1,0:T(8,128)S(1)}, ...), branch_computations={%region_1.2_spmd, %region_2.3_spmd, %region_3.4_spmd, %region_4.5_... | conditional | flops 1000000000 | bytes 21859900 | solution.py:777
  57.5 0.1 collective-permute-start.2
  57.6 3.8 %gather.14 = (f32[4,896,128]{2,1,0:T(8,128)S(1)}, f32[4,640,128]{2,1,0:T(8,128)S(1)}) custom-call(s32[33]{0:T(128)S(1)} %get-tuple-element.256.order, f32[10,384,128]{2,1,0:T(8,128)S(1)} %get-tuple-element.257.rem, f32[6,224,128]{2,1,0:T(8,128)S(1)} %get-tuple-element.258.s_head, f32[6,160,128]{2,1,0:T(8,128)} %get-tuple-element.259.got_p, ...), custom_call_target="tpu_custom_call" | custom-call | flops 1000000000 | bytes 6000000 | tf_op jit(solution)/shard_map/cond/branch_3_fun/gather/pallas_call | solution.py:743
  61.4 19.5 %collective-permute-done.2.refs_0_ = f32[3,384,128]{2,1,0:T(8,128)S(1)} collective-permute-done((f32[3,384,128]{2,1,0:T(8,128)S(1)}, f32[3,384,128]{2,1,0:T(8,128)S(1)}, u32[]{:S(2)}, u32[]{:S(2)}) %collective-permute-start.2) | collective-permute-done | bytes 589856 | tf_op jit(solution)/shard_map/cond/branch_3_fun/ppermute | solution.py:742
  81.0 2.4 %finish.14 = (f32[4,896,128]{2,1,0:T(8,128)}, f32[4,640,128]{2,1,0:T(8,128)}) custom-call(s32[33]{0:T(128)S(1)} %get-tuple-element.256.order, f32[4,896,128]{2,1,0:T(8,128)S(1)} %get-tuple-element.266.near_s, f32[4,640,128]{2,1,0:T(8,128)S(1)} %get-tuple-element.267.near_p, f32[3,384,128]{2,1,0:T(8,128)S(1)} %collective-permute-done.2.refs_0_), custom_call_target="tpu_custom_call" | custom-call | tf_op jit(solution)/shard_map/cond/branch_3_fun/finish/pallas_call | solution.py:758
  (2 shorter events, 0.0 us)
Async XLA Ops:
  3.3 50.8 %collective-permute-start.12 = (f32[6,160,128]{2,1,0:T(8,128)}, f32[6,160,128]{2,1,0:T(8,128)}, u32[]{:S(2)}, u32[]{:S(2)}) collective-permute-start(f32[6,160,128]{2,1,0:T(8,128)} %get-tuple-element.380), channel_id=1, source_target_pairs={{8,0},{9,1},{10,2},{11,3},{12,4},{13,5},{14,6},{15,7},{0,8},{1,9},... | collective-permute-start | bytes 1474568 | tf_op jit(solution)/shard_map/ppermute | solution.py:670
  27.3 30.2 %collective-permute-start.13 = (f32[6,224,128]{2,1,0:T(8,128)S(1)}, f32[6,224,128]{2,1,0:T(8,128)S(1)}, u32[]{:S(2)}, u32[]{:S(2)}) collective-permute-start(f32[6,224,128]{2,1,0:T(8,128)S(1)} %get-tuple-element.379), channel_id=1, source_target_pairs={{8,0},{9,1},{10,2},{11,3},{12,4},{13,5},{14,6},{15,7},{0,8},{1,9},... | collective-permute-start | bytes 2064392 | tf_op jit(solution)/shard_map/ppermute | solution.py:714
  27.7 21.3 %copy-start.34 = (f32[8,128]{1,0:T(8,128)S(1)}, f32[8,128]{1,0:T(8,128)}, u32[]{:S(2)}) copy-start(f32[8,128]{1,0:T(8,128)} %get-tuple-element.373) | copy-start | bytes 12292
  27.7 22.1 %copy-start.35 = (f32[6]{0:T(128)S(1)}, f32[6]{0:T(128)}, u32[]{:S(2)}) copy-start(f32[6]{0:T(128)} %constant.42.clone) | copy-start | bytes 76
  27.7 22.1 %copy-start.31 = (f32[8,6,24]{2,1,0:T(8,128)S(1)}, f32[8,6,24]{2,1,0:T(8,128)}, u32[]{:S(2)}) copy-start(f32[8,6,24]{2,1,0:T(8,128)} %constant.37.clone.bmat) | copy-start | bytes 13828
  27.7 22.3 %copy-start.32 = (f32[23,36]{1,0:T(8,128)S(1)}, f32[23,36]{1,0:T(8,128)}, u32[]{:S(2)}) copy-start(f32[23,36]{1,0:T(8,128)} %constant.41.clone) | copy-start | bytes 9940
  27.7 23.9 %copy-start.33 = (s32[4,4]{1,0:T(4,128)S(1)}, s32[4,4]{1,0:T(4,128)}, u32[]{:S(2)}) copy-start(s32[4,4]{1,0:T(4,128)} %flag.1) | copy-start | bytes 196
  49.8 7.7 %copy-start.30 = (f32[16,128]{1,0:T(8,128)}, f32[16,128]{1,0:T(8,128)S(1)}, u32[]{:S(2)}) copy-start(f32[16,128]{1,0:T(8,128)S(1)} %fusion.7) | copy-start | bytes 24580
  50.0 2.9 %collective-permute-start.10 = (f32[4,24]{1,0:T(4,128)S(1)}, f32[4,24]{1,0:T(4,128)S(1)}, u32[]{:S(2)}, u32[]{:S(2)}) collective-permute-start(f32[4,24]{1,0:T(4,128)S(1)} %fusion.1), channel_id=1, source_target_pairs={{16,0},{0,16},{17,1},{1,17},{18,2},{2,18},{19,3},{3,19},{20,4},{4,... | collective-permute-start | bytes 1160 | tf_op jit(solution)/shard_map/ppermute | solution.py:728
  51.0 2.5 %collective-permute-start.11 = (f32[4,576]{1,0:T(4,128)S(1)}, f32[4,576]{1,0:T(4,128)S(1)}, u32[]{:S(2)}, u32[]{:S(2)}) collective-permute-start(f32[4,576]{1,0:T(4,128)S(1)} %div.18), channel_id=1, source_target_pairs={{16,0},{0,16},{17,1},{1,17},{18,2},{2,18},{19,3},{3,19},{20,4},{4,... | collective-permute-start | bytes 27656 | tf_op jit(solution)/shard_map/ppermute | solution.py:729
  57.5 23.4 %collective-permute-start.2 = (f32[3,384,128]{2,1,0:T(8,128)S(1)}, f32[3,384,128]{2,1,0:T(8,128)S(1)}, u32[]{:S(2)}, u32[]{:S(2)}) collective-permute-start(f32[3,384,128]{2,1,0:T(8,128)S(1)} %slice.26), channel_id=1, source_target_pairs={{8,0},{9,1},{10,2},{11,3},{12,4},{13,5},{14,6},{15,7},{0,8},{1,9},... | collective-permute-start | bytes 1769480 | tf_op jit(solution)/shard_map/cond/branch_3_fun/ppermute | solution.py:742

commit v3 on v1

--- a/solution.py
+++ b/solution.py
@@ -18,11 +18,12 @@
 SLOPE = 0.05
 top_precision = lax.Precision.HIGHEST
 SUMS = 29
+PAIRS = 2
 LINES = GRID * PLANE // LANES
 P_ROWS = 5 * LINES
 S_ROWS = 7 * LINES
 ROWS = P_ROWS + S_ROWS
-EARLY = 6
+EARLY = 7
 
 
 def strain_table():
@@ -155,8 +156,7 @@
     field,
     work,
     spec,
-    part_hi,
-    part_lo,
+    parts,
     acc,
 ):
     total = elems * points
@@ -276,7 +276,19 @@
         inc = jnp.where(second, newton(over, inc, mu3, rest, rate), inc)
         return jnp.where(third, newton(over, inc, mu3, rest, rate), inc)
 
-    def stress_step(pair, carry):
+    def split_rows(comp):
+        if comp < 3:
+            return comp * block, (3 + comp) * block
+        return 2 * comp * block, (2 * comp + 1) * block
+
+    def split_store(comp, pair, half, value):
+        upper = value.astype(jnp.bfloat16)
+        lower = (value - upper.astype(jnp.float32)).astype(jnp.bfloat16)
+        lanes = slice(half * LANES, (half + 1) * LANES)
+        for base, part in zip(split_rows(comp), (upper, lower)):
+            parts[pl.ds(base + pair * 16, 16), lanes] = part
+
+    def stress_pair(pair):
         for half in range(2):
             load, volume, mu, dev, squared = trial(half, pair)
             base = load(9)
@@ -290,42 +302,37 @@
                 value = shrink * dev[comp]
                 if comp < 3:
                     value = value + pressure
-                upper = value.astype(jnp.bfloat16)
-                at = pl.ds(comp * block + pair * 16, 16)
-                lanes = slice(half * LANES, (half + 1) * LANES)
-                part_hi[at, lanes] = upper
-                part_lo[at, lanes] = (value - upper.astype(jnp.float32)).astype(jnp.bfloat16)
+                split_store(comp, pair, half, value)
+
+    def stress_step(step, carry):
+        for near in range(PAIRS):
+            stress_pair(step * PAIRS + near)
         return carry
 
     def plane_product(store):
-        for which, (from_row, rows) in enumerate(
-            ((0, 3 * block), (3 * block, block), (4 * block, block), (5 * block, block))
-        ):
-            for at in range(from_row, from_row + rows, block):
-                left_hi = part_hi[at : at + block, :]
-                left_lo = part_lo[at : at + block, :]
-                dot = functools.partial(jnp.dot, preferred_element_type=jnp.float32)
-                store(
-                    at,
-                    dot(left_hi, high[which])
-                    + (dot(left_lo, high[which]) + dot(left_hi, low[which])),
-                )
+        dot = functools.partial(jnp.dot, preferred_element_type=jnp.float32)
+        for which, comps in enumerate(((0, 1, 2), (3,), (4,), (5,))):
+            from_row, rows = split_rows(comps[0])[0], len(comps) * block
+            both = dot(parts[from_row : from_row + 2 * rows, :], high[which])
+            rest = dot(parts[from_row : from_row + rows, :], low[which])
+            store(comps[0] * block, both[:rows] + (both[rows:] + rest))
 
     def store_spec(at, value):
         for half in range(2):
-            work[half, at : at + block, :] = value[:, half * LANES : (half + 1) * LANES]
+            work[half, at : at + value.shape[0], :] = value[:, half * LANES : (half + 1) * LANES]
 
     def update_field(at, value):
         for half in range(2):
-            field[half, at : at + block, :] = (
-                field[half, at : at + block, :] - value[:, half * LANES : (half + 1) * LANES]
+            field[half, at : at + value.shape[0], :] = (
+                field[half, at : at + value.shape[0], :]
+                - value[:, half * LANES : (half + 1) * LANES]
             )
 
     def flip(comp, k):
         return (-k) % GRID if comp in (4, 5) else k
 
     def sweep(index, carry):
-        lax.fori_loop(0, GRID // 2, stress_step, 0)
+        lax.fori_loop(0, GRID // (2 * PAIRS), stress_step, 0)
         plane_product(store_spec)
         scale_cell = jnp.where(index < fft_count, inv_mu, 0.0)
 
@@ -383,13 +390,7 @@
                 )
                 for pair in range(GRID // 2):
                     value = jnp.concatenate([lines[2 * pair], lines[2 * pair + 1]], axis=0)
-                    upper = value.astype(jnp.bfloat16)
-                    at = comp * block + pair * 16
-                    lanes = slice(half * LANES, (half + 1) * LANES)
-                    part_hi[at : at + 16, lanes] = upper
-                    part_lo[at : at + 16, lanes] = (value - upper.astype(jnp.float32)).astype(
-                        jnp.bfloat16
-                    )
+                    split_store(comp, pair, half, value)
         plane_product(update_field)
         return carry
 
@@ -658,8 +659,7 @@
                 pltpu.VMEM((2, 6 * block, LANES), jnp.float32),
                 pltpu.VMEM((2, 6 * block, LANES), jnp.float32),
                 pltpu.VMEM((2, 6 * block, LANES), jnp.float32),
-                pltpu.VMEM((6 * block, PLANE), jnp.bfloat16),
-                pltpu.VMEM((6 * block, PLANE), jnp.bfloat16),
+                pltpu.VMEM((2 * 6 * block, PLANE), jnp.bfloat16),
                 pltpu.VMEM((SUMS, BATCH, LANES), jnp.float32),
             ],
             compiler_params=params,

time: 132 us -> 105 us (0.80)
  waiting for transfers between devices: 67.5 us -> 41.5 us
  Pallas kernels: 51.4 us -> 49.9 us
    ppermute x1, waiting for transfers between devices: 67.4 us -> 41.5 us  [run(): got = lax.ppermute(cells[:count], 'cell', route)]
    ppermute x1, starting transfers between devices: 2.64 us -> 0.38 us  [local(): got_p = lax.ppermute(p_head, 'cell', route)]
    ppermute x1, starting transfers between devices: 0.33 us -> 2.59 us  [local(): got_s = lax.ppermute(s_head, 'cell', route)]
    pallas_call x2, Pallas kernels: 45 us -> 43.6 us  [solve(): pl.pallas_call(functools.partial(solve_kernel, elems, points, begin, firs...]
  transfers between devices with their start and end apart: 5 -> 5, of which waited for: 1 -> 1; matrix products, arithmetic and copies ran while one was open for 4% -> 6% of each run, Pallas kernels for 0% -> 21%
where the time goes in v3:
time: 105 us
  Pallas kernels  49.9 us (48%)
  waiting for transfers between devices  41.5 us (40%)
  starting transfers between devices  5.88 us (6%)
  local copies, waits for them, and re-layouts  2.17 us (2%)
  matrix products  1.86 us (2%)
  other arithmetic  1.82 us (2%)
  between operations  1.45 us (1%)
    pallas_call x2, Pallas kernels, solve(): pl.pallas_call(functools.partial(solve_kernel, elems, points, begin, firs...  43.6 us
    ppermute x1, waiting for transfers between devices, run(): got = lax.ppermute(cells[:count], 'cell', route)  41.5 us
    pallas_call x1, Pallas kernels, local(): pl.pallas_call(functools.partial(merge_kernel, elems, points, first), out...  3.63 us
    pallas_call x1, Pallas kernels, local(): pl.pallas_call(functools.partial(pack_kernel, elems, points, first), out_...  2.73 us
    ppermute x1, starting transfers between devices, run(): got = lax.ppermute(cells[:count], 'cell', route)  2.66 us
    ppermute x1, starting transfers between devices, local(): got_s = lax.ppermute(s_head, 'cell', route)  2.59 us
  transfers between devices with their start and end apart: 5, of which 1 were waited for; matrix products, arithmetic and copies ran while one was open for 6% of the time, Pallas kernels for 21%

profile of v3, /device:TPU:2, one launch (start us, length us, event | category | flops | bytes accessed | tf_op | source)
XLA Modules:
  0.0 104.6 jit_solution(10838069539236971624)
XLA Ops:
  0.6 2.7 %pack.1 = (s32[33]{0:T(128)}, f32[7,160,128]{2,1,0:T(8,128)}) custom-call(s32[4,4]{1,0:T(4,128)} %flag.1, f32[512,128]{1,0:T(8,128)} %bitcast.69, f32[512,128]{1,0:T(8,128)} %bitcast.73, f32[512,128]{1,0:T(8,128)} %bitcast.77, f32[512,128]{1,0:T(8,128)} %bitcast.81, f32[512,128]{1,0:T(8,128)} %bitcast.85), custom_call_target="tpu_custom_call" | custom-call | tf_op jit(solution)/shard_map/pack/pallas_call | solution.py:633
  3.4 21.5 %solve.2 = (f32[7,224,128]{2,1,0:T(8,128)}, f32[1,384,128]{2,1,0:T(8,128)}, f32[8,128]{1,0:T(8,128)}) custom-call(s32[33]{0:T(128)} %get-tuple-element.39.order, s32[4,4]{1,0:T(4,128)} %fft_iters.3, s32[4,4]{1,0:T(4,128)} %rm_iters.3, f32[4,1,24]{2,1,0:T(1,128)} %bitcast.98, f32[8,6,24]{2,1,0:T(8,128)} %constant.53.clone.bmat, f32[3072,128]{1,0:T(8,128)} %bitcast.93, ...), custom_call_target="tpu_custom_call" | custom-call | flops 20000000000 | bytes 8000000 | tf_op jit(solution)/shard_map/solve/pallas_call | solution.py:652
  24.9 2.6 %collective-permute-start.12 = (f32[7,224,128]{2,1,0:T(8,128)}, f32[7,224,128]{2,1,0:T(8,128)S(1)}, u32[]{:S(2)}, u32[]{:S(2)}) collective-permute-start(f32[7,224,128]{2,1,0:T(8,128)} %get-tuple-element.48.s_head), channel_id=1, source_target_pairs={{8,0},{9,1},{10,2},{11,3},{12,4},{13,5},{14,6},{15,7},{0,8},{1,9},... | collective-permute-start | bytes 2408456 | tf_op jit(solution)/shard_map/ppermute | solution.py:686
  27.4 0.0 copy-start.6
  27.4 0.0 copy-start.11
  27.4 0.0 copy-start.12
  27.5 0.0 copy-start.8
  27.5 0.0 copy-start.9
  27.5 0.0 copy-start.10
  27.5 22.1 %solve.3 = (f32[9,384,128]{2,1,0:T(8,128)}, f32[8,128]{1,0:T(8,128)}) custom-call(s32[33]{0:T(128)} %get-tuple-element.39.order, s32[4,4]{1,0:T(4,128)} %fft_iters.3, s32[4,4]{1,0:T(4,128)} %rm_iters.3, f32[4,1,24]{2,1,0:T(1,128)} %bitcast.99, f32[8,6,24]{2,1,0:T(8,128)} %constant.53.clone.bmat, f32[3072,128]{1,0:T(8,128)} %bitcast.94, f32[512,128]{1,0:T(8,128)} %bitcast.97, ...), custom_call_target="tpu_custom_call" | custom-call | flops 20000000000 | bytes 8000000 | tf_op jit(solution)/shard_map/solve/pallas_call | solution.py:652
  49.6 0.0 copy-done.6
  49.6 0.0 copy-done.11
  49.6 0.8 fusion.7
  50.4 0.0 copy-done.12
  50.4 0.0 copy-done.8
  50.4 0.2 fusion.1
  50.6 0.0 collective-permute-start.9
  50.6 0.4 collective-permute-start.11
  51.0 0.0 copy-done.9
  51.0 0.2 fusion.5
  51.2 0.1 reshape.94
  51.3 0.4 convolution_bitcast_fusion
  51.7 0.3 fusion
  52.0 0.1 div.18
  52.0 0.3 collective-permute-start.10
  52.3 0.0 copy-done.10
  52.3 0.6 convert_reduce_fusion
  53.6 0.0 collective-permute-done.9
  53.6 0.6 add.11
  54.2 0.0 collective-permute-done.10
  54.2 0.6 add.12
  54.8 0.0 copy-start.4
  54.8 0.0 copy-start.5
  54.8 0.0 copy-done.7
  54.8 46.1 %conditional.1 = (f32[9,384,128]{2,1,0:T(8,128)}) conditional(s32[]{:T(128)} %clamp.3, f32[9,384,128]{2,1,0:T(8,128)} %get-tuple-element.47, f32[9,384,128]{2,1,0:T(8,128)} %get-tuple-element.47, f32[9,384,128]{2,1,0:T(8,128)} %get-tuple-element.47, f32[9,384,128]{2,1,0:T(8,128)} %get-tuple-element.47, ...), branch_computations={%region_1.2_spmd, %region_2.3_spmd, %region_3.4_spmd, %region_4.5_... | conditional | bytes 12582960 | solution.py:716
  54.9 1.2 %slice.23 = f32[2,384,128]{2,1,0:T(8,128)S(1)} slice(f32[9,384,128]{2,1,0:T(8,128)} %param.2), slice={[0:2], [0:384], [0:128]} | slice | bytes 786432 | tf_op jit(solution)/shard_map/cond/branch_2_fun/slice | solution.py:708
  56.0 2.7 %collective-permute-start.2 = (f32[2,384,128]{2,1,0:T(8,128)S(1)}, f32[2,384,128]{2,1,0:T(8,128)S(1)}, u32[]{:S(2)}, u32[]{:S(2)}) collective-permute-start(f32[2,384,128]{2,1,0:T(8,128)S(1)} %slice.23), channel_id=1, source_target_pairs={{8,0},{9,1},{10,2},{11,3},{12,4},{13,5},{14,6},{15,7},{0,8},{1,9},... | collective-permute-start | bytes 1179656 | tf_op jit(solution)/shard_map/cond/branch_2_fun/ppermute | solution.py:708
  58.7 41.5 %collective-permute-done.2 = f32[2,384,128]{2,1,0:T(8,128)S(1)} collective-permute-done((f32[2,384,128]{2,1,0:T(8,128)S(1)}, f32[2,384,128]{2,1,0:T(8,128)S(1)}, u32[]{:S(2)}, u32[]{:S(2)}) %collective-permute-start.2) | collective-permute-done | bytes 393248 | tf_op jit(solution)/shard_map/cond/branch_2_fun/ppermute | solution.py:708
  100.1 0.8 constant_dynamic-update-slice_fusion.1
  100.9 0.0 collective-permute-done.11.got_p
  100.9 0.0 collective-permute-done.12.got_s
  100.9 0.0 copy-done
  100.9 0.0 copy-done.1
  101.0 0.0 copy-done.2
  101.0 0.0 copy-done.3
  101.0 0.0 copy-done.4
  101.0 0.0 copy-done.5
  101.0 3.6 %merge.1 = (f32[4,896,128]{2,1,0:T(8,128)}, f32[4,640,128]{2,1,0:T(8,128)}) custom-call(s32[33]{0:T(128)S(1)} %copy-done.6, f32[9,384,128]{2,1,0:T(8,128)} %get-tuple-element.52.rem, f32[7,224,128]{2,1,0:T(8,128)S(1)} %copy-done.5, f32[7,160,128]{2,1,0:T(8,128)S(1)} %collective-permute-done.11.got_p, f32[7,224,128]{2,1,0:T(8,128)S(1)} %collective-permute-done.12.got_s, ...), custom_call_target="tpu_custom_call" | custom-call | tf_op jit(solution)/shard_map/merge/pallas_call | solution.py:718
  (6 shorter events, 0.0 us)
Async XLA Ops:
  24.9 76.1 %collective-permute-start.12 = (f32[7,224,128]{2,1,0:T(8,128)}, f32[7,224,128]{2,1,0:T(8,128)S(1)}, u32[]{:S(2)}, u32[]{:S(2)}) collective-permute-start(f32[7,224,128]{2,1,0:T(8,128)} %get-tuple-element.48.s_head), channel_id=1, source_target_pairs={{8,0},{9,1},{10,2},{11,3},{12,4},{13,5},{14,6},{15,7},{0,8},{1,9},... | collective-permute-start | bytes 2408456 | tf_op jit(solution)/shard_map/ppermute | solution.py:686
  27.4 22.1 %copy-start.6 = (s32[33]{0:T(128)S(1)}, s32[33]{0:T(128)}, u32[]{:S(2)}) copy-start(s32[33]{0:T(128)} %get-tuple-element.39.order) | copy-start | bytes 400
  27.4 22.1 %copy-start.11 = (f32[8,128]{1,0:T(8,128)S(1)}, f32[8,128]{1,0:T(8,128)}, u32[]{:S(2)}) copy-start(f32[8,128]{1,0:T(8,128)} %get-tuple-element.42) | copy-start | bytes 12292
  27.4 22.9 %copy-start.12 = (f32[6]{0:T(128)S(1)}, f32[6]{0:T(128)}, u32[]{:S(2)}) copy-start(f32[6]{0:T(128)} %constant.58.clone) | copy-start | bytes 76
  27.5 23.0 %copy-start.8 = (f32[8,6,24]{2,1,0:T(8,128)S(1)}, f32[8,6,24]{2,1,0:T(8,128)}, u32[]{:S(2)}) copy-start(f32[8,6,24]{2,1,0:T(8,128)} %constant.53.clone.bmat) | copy-start | bytes 13828
  27.5 23.6 %copy-start.9 = (f32[23,36]{1,0:T(8,128)S(1)}, f32[23,36]{1,0:T(8,128)}, u32[]{:S(2)}) copy-start(f32[23,36]{1,0:T(8,128)} %constant.57.clone) | copy-start | bytes 9940
  27.5 24.8 %copy-start.10 = (s32[4,4]{1,0:T(4,128)S(1)}, s32[4,4]{1,0:T(4,128)}, u32[]{:S(2)}) copy-start(s32[4,4]{1,0:T(4,128)} %flag.1) | copy-start | bytes 196
  50.4 4.4 %copy-start.7 = (f32[16,128]{1,0:T(8,128)}, f32[16,128]{1,0:T(8,128)S(1)}, u32[]{:S(2)}) copy-start(f32[16,128]{1,0:T(8,128)S(1)} %fusion.7) | copy-start | bytes 24580
  50.6 3.0 %collective-permute-start.9 = (f32[4,24]{1,0:T(4,128)S(1)}, f32[4,24]{1,0:T(4,128)S(1)}, u32[]{:S(2)}, u32[]{:S(2)}) collective-permute-start(f32[4,24]{1,0:T(4,128)S(1)} %fusion.1), channel_id=1, source_target_pairs={{16,0},{0,16},{17,1},{1,17},{18,2},{2,18},{19,3},{3,19},{20,4},{4,... | collective-permute-start | bytes 1160 | tf_op jit(solution)/shard_map/ppermute | solution.py:700
  50.6 50.3 %collective-permute-start.11 = (f32[7,160,128]{2,1,0:T(8,128)}, f32[7,160,128]{2,1,0:T(8,128)S(1)}, u32[]{:S(2)}, u32[]{:S(2)}) collective-permute-start(f32[7,160,128]{2,1,0:T(8,128)} %get-tuple-element.49), channel_id=1, source_target_pairs={{8,0},{9,1},{10,2},{11,3},{12,4},{13,5},{14,6},{15,7},{0,8},{1,9},... | collective-permute-start | bytes 1720328 | tf_op jit(solution)/shard_map/ppermute | solution.py:642
  52.0 2.1 %collective-permute-start.10 = (f32[4,576]{1,0:T(4,128)S(1)}, f32[4,576]{1,0:T(4,128)S(1)}, u32[]{:S(2)}, u32[]{:S(2)}) collective-permute-start(f32[4,576]{1,0:T(4,128)S(1)} %div.18), channel_id=1, source_target_pairs={{16,0},{0,16},{17,1},{1,17},{18,2},{2,18},{19,3},{3,19},{20,4},{4,... | collective-permute-start | bytes 27656 | tf_op jit(solution)/shard_map/ppermute | solution.py:701
  54.8 46.1 %copy-start = (f32[4,4,4096]{2,1,0:T(4,128)S(1)}, f32[4,4,4096]{2,1,0:T(4,128)}, u32[]{:S(2)}) copy-start(f32[4,4,4096]{2,1,0:T(4,128)} %param.31) | copy-start | bytes 786436
  54.8 46.2 %copy-start.1 = (f32[4,4,4096]{2,1,0:T(4,128)S(1)}, f32[4,4,4096]{2,1,0:T(4,128)}, u32[]{:S(2)}) copy-start(f32[4,4,4096]{2,1,0:T(4,128)} %param.32) | copy-start | bytes 786436
  54.8 46.2 %copy-start.2 = (f32[4,4,4096]{2,1,0:T(4,128)S(1)}, f32[4,4,4096]{2,1,0:T(4,128)}, u32[]{:S(2)}) copy-start(f32[4,4,4096]{2,1,0:T(4,128)} %param.33) | copy-start | bytes 786436
  54.8 46.2 %copy-start.3 = (f32[4,4,4096]{2,1,0:T(4,128)S(1)}, f32[4,4,4096]{2,1,0:T(4,128)}, u32[]{:S(2)}) copy-start(f32[4,4,4096]{2,1,0:T(4,128)} %param.34) | copy-start | bytes 786436
  54.8 46.2 %copy-start.4 = (f32[4,4,4096]{2,1,0:T(4,128)S(1)}, f32[4,4,4096]{2,1,0:T(4,128)}, u32[]{:S(2)}) copy-start(f32[4,4,4096]{2,1,0:T(4,128)} %param.35) | copy-start | bytes 786436
  54.8 46.2 %copy-start.5 = (f32[7,224,128]{2,1,0:T(8,128)S(1)}, f32[7,224,128]{2,1,0:T(8,128)}, u32[]{:S(2)}) copy-start(f32[7,224,128]{2,1,0:T(8,128)} %get-tuple-element.48.s_head) | copy-start | bytes 2408452
  56.0 44.1 %collective-permute-start.2 = (f32[2,384,128]{2,1,0:T(8,128)S(1)}, f32[2,384,128]{2,1,0:T(8,128)S(1)}, u32[]{:S(2)}, u32[]{:S(2)}) collective-permute-start(f32[2,384,128]{2,1,0:T(8,128)S(1)} %slice.23), channel_id=1, source_target_pairs={{8,0},{9,1},{10,2},{11,3},{12,4},{13,5},{14,6},{15,7},{0,8},{1,9},... | collective-permute-start | bytes 1179656 | tf_op jit(solution)/shard_map/cond/branch_2_fun/ppermute | solution.py:708
